TPU v7x, 32 devices: a whole 2x2x4 slice. The times are simulated.
32 devices in a mesh: seq: 8 (over y, x, core), grp: 4 (over z).
Axes of the slice: x: 2, y: 2, z: 4, core: 2. Of those that a mesh axis runs over, the one named last changes fastest.
Arguments:
- tokens: bfloat16 [4, 8192, 3072], P('grp', 'seq'), may hold values from -24 to 24
- block_map: int32 [4, 64], P('grp', 'seq'), may hold values from 0 to 1, as said below
- slot_keys: bfloat16 [3072, 128], replicated, may hold values from -2 to 2
- gate_weight: bfloat16 [8, 3072, 4096], P('grp', None, 'seq'), may hold values from -0.109375 to 0.109375
- up_weight: bfloat16 [8, 3072, 4096], P('grp', None, 'seq'), may hold values from -0.109375 to 0.109375
- down_weight: bfloat16 [8, 4096, 3072], P('grp', 'seq'), may hold values from -0.09375 to 0.09375
Outputs:
- mixed: bfloat16 [4, 8192, 3072], P('grp', 'seq')
Inputs may be any that keep to these rules, and one draw needn't show every extreme that they name: `block_map`: every sequence has at least one image block and at least one text block.
All inputs are finite; a program needn't handle non-finite values.
Results may differ from a plain program's by a relative error of at most 0.014.
Values may be sent and summed in bfloat16 or wider, within the bound.
No kernel may reach another device: no remote copies, remote signals or barrier semaphores. Data moves between devices by JAX's collectives and lax.ppermute only.
A program may use at most 128 MiB of HBM per device.

v0:
```python
import jax
import jax.numpy as jnp
from jax import lax
from jax.sharding import PartitionSpec as P

BLOCK = 128


def body(tokens, block_map, slot_keys, gate_weight, up_weight, down_weight):
    seq_tokens = tokens[0]
    rows_here = seq_tokens.shape[0]
    slot_count = slot_keys.shape[1]
    groups = lax.axis_size("grp")
    exp_dev = gate_weight.shape[0]
    per_expert = slot_count // (groups * exp_dev)
    image_slots = 3 * slot_count // 4
    slot_text = (jnp.arange(slot_count) >= image_slots).astype(jnp.int32)
    block_total = block_map.shape[1]
    allowed = block_map[0][:, None, None] == slot_text[None, None, :]
    allowed = jnp.broadcast_to(allowed, (block_total, BLOCK, slot_count)).reshape(
        rows_here, slot_count
    )
    logits = jnp.dot(seq_tokens, slot_keys, preferred_element_type=jnp.float32)
    masked = jnp.where(allowed, logits, -1e30)
    local_peak = jnp.max(masked, axis=0)
    global_peak = lax.pmax(local_peak, "seq")
    weights = jnp.where(allowed, jnp.exp(masked - global_peak[None, :]), 0.0)
    totals_loc = jnp.sum(weights, axis=0)
    rows_loc = jnp.einsum(
        "ts,td->sd", weights.astype(jnp.bfloat16), seq_tokens, preferred_element_type=jnp.float32
    )
    totals_loc, rows_loc = (totals_loc, rows_loc)
    rows_part = lax.psum_scatter(rows_loc, "seq", scatter_dimension=1, tiled=True)
    totals = lax.psum(totals_loc, "seq")
    slot_part = (rows_part / totals[:, None]).astype(jnp.bfloat16)
    col_width = slot_part.shape[1]
    arrived = lax.all_to_all(
        slot_part.reshape(groups, slot_count // groups, col_width),
        "grp",
        split_axis=0,
        concat_axis=0,
        tiled=True,
    )
    arrived = arrived.reshape(groups, exp_dev, per_expert, col_width)
    columns_in = lax.all_gather(arrived, "seq", axis=3, tiled=True)
    gate_more = jnp.einsum(
        "gesd,edf->gesf", columns_in, gate_weight, preferred_element_type=jnp.float32
    )
    up_more = jnp.einsum(
        "gesd,edf->gesf", columns_in, up_weight, preferred_element_type=jnp.float32
    )
    hidden = (jax.nn.silu(gate_more) * up_more).astype(jnp.bfloat16)
    partial_value = jnp.einsum(
        "gesf,efd->gesd", hidden, down_weight, preferred_element_type=jnp.float32
    )
    owned_part = lax.psum_scatter(partial_value, "seq", scatter_dimension=3, tiled=True).astype(
        jnp.bfloat16
    )
    returned = lax.all_to_all(owned_part, "grp", split_axis=0, concat_axis=0, tiled=True)
    row_peak = jnp.max(masked, axis=1)
    scores = jnp.where(allowed, jnp.exp(masked - row_peak[:, None]), 0.0)
    mix_weights = (scores / jnp.sum(scores, axis=1)[:, None]).astype(jnp.bfloat16)
    columns_in = lax.all_gather(returned, "seq", axis=3, tiled=True)
    flat_slots = columns_in.reshape(slot_count, columns_in.shape[3])
    output = jnp.dot(mix_weights, flat_slots, preferred_element_type=jnp.float32)
    return output.astype(jnp.bfloat16)[None]


def solution(mesh):
    placed = (
        P("grp", "seq", None),
        P("grp", "seq"),
        P(),
        P("grp", None, "seq"),
        P("grp", None, "seq"),
        P("grp", "seq", None),
    )
    return jax.shard_map(
        body, mesh=mesh, in_specs=placed, out_specs=P("grp", "seq", None), check_vma=False
    )
```

profile of v0, /device:TPU:0, one launch (start us, length us, event | category | flops | bytes accessed | tf_op | source)
XLA Modules:
  0.0 175.4 jit_solution(14218418531017344007)
XLA Ops:
  6.5 0.0 copy-start
  6.5 0.0 reduce-scatter.3.cloned.1.call-start
  6.5 0.8 broadcast_compare_fusion
  7.4 0.3 copy-done
  7.7 4.6 %fusion.34 = (f32[128]{0:T(128)S(1)}, f32[1024]{0:T(1024)S(1)}, f32[1024,128]{1,0:T(8,128)S(1)}) fusion(pred[1024,128]{1,0:T(32,128)(4,1)S(1)} %bitcast.74, bf16[3072,128]{1,0:T(8,128)(2,1)S(1)} %copy-done, bf16[1,1024,3072]{2,1,0:T(8,128)(2,1)} %param.6), kind=kOutput, calls=%fused_computation.27 | convolution fusion | flops 805698432 | bytes 7737856 | tf_op jit(solution)/shard_map/dot_general | solution.py:23
  12.3 15.2 %pmax.7 = f32[128]{0:T(128)S(1)} all-reduce(f32[128]{0:T(128)S(1)} %get-tuple-element.7), channel_id=1, replica_groups=mesh['seq'=8,'grp'=4] {'seq'}, use_global_device_ids=true, to_apply=%region_3.4 | all-reduce | flops 128 | bytes 1024 | tf_op jit(solution)/shard_map/pmax | solution.py:26
  27.5 0.4 fusion.29
  27.8 5.0 %fusion.6 = f32[128,3072]{1,0:T(8,128)} fusion(bf16[1024,128]{1,0:T(8,128)(2,1)S(1)} %get-tuple-element.9, bf16[1,1024,3072]{2,1,0:T(8,128)(2,1)} %param.6), kind=kOutput, calls=%fused_computation.6 | convolution fusion | flops 805306368 | bytes 8126464 | tf_op jit(solution)/shard_map/ts,td->sd/dot_general | solution.py:29
  32.8 0.0 reduce-scatter.3.cloned.1.call-update
  32.8 0.0 reduce-scatter.5.cloned.1.call-start
  32.9 11.8 %psum.7 = f32[128]{0:T(128)S(1)} all-reduce(f32[128]{0:T(128)S(1)} %get-tuple-element.5), channel_id=1, replica_groups=mesh['seq'=8,'grp'=4] {'seq'}, use_global_device_ids=true, to_apply=%region_6.7 | all-reduce | flops 128 | bytes 1024 | tf_op jit(solution)/shard_map/psum | solution.py:34
  44.7 26.0 %reduce-scatter.3.cloned.1.call-done = f32[128,384]{1,0:T(8,128)} async-done(((f32[128,3072]{1,0:T(8,128)}), f32[128,384]{1,0:T(8,128)}) %reduce-scatter.3.cloned.1.call-update) | async-done | bytes 196624 | tf_op jit(solution)/shard_map/reduce_scatter | solution.py:33
  70.7 1.0 divide_convert_fusion.1
  71.7 10.2 %all_to_all.10 = bf16[4,32,384]{2,1,0:T(8,128)(2,1)S(1)} all-to-all(bf16[4,32,384]{2,1,0:T(8,128)(2,1)S(1)} %bitcast.73), channel_id=1, replica_groups=mesh['seq'=8,'grp'=4] {'grp'}, dimensions={0} | all-to-all | bytes 196608 | tf_op jit(solution)/shard_map/all_to_all | solution.py:37
  82.0 10.9 %all_gather.6 = bf16[4,2,16,3072]{3,2,0,1:T(8,128)(2,1)S(1)} all-gather(bf16[4,2,16,384]{3,2,0,1:T(8,128)(2,1)S(1)} %copy.9), channel_id=1, replica_groups=mesh['seq'=8,'grp'=4] {'seq'}, dimensions={3}, use_global_device_ids=true | all-gather | bytes 884736 | tf_op jit(solution)/shard_map/all_gather | solution.py:45
  92.9 4.0 %fusion.16 = f32[4,2,16,512]{3,2,0,1:T(8,128)S(1)} fusion(bf16[4,2,16,3072]{3,2,0,1:T(8,128)(2,1)S(1)} %all_gather.6, bf16[2,3072,512]{2,1,0:T(8,128)(2,1)} %param.9), kind=kOutput, calls=%fused_computation.13 | convolution fusion | flops 402653184 | bytes 7340032 | tf_op jit(solution)/shard_map/gesd,edf->gesf/dot_general | solution.py:46
  96.8 8.0 %fusion.10 = f32[4,2,16,3072]{3,2,0,1:T(8,128)} fusion(bf16[2,512,3072]{2,1,0:T(8,128)(2,1)} %param.11, bf16[4,2,16,3072]{3,2,0,1:T(8,128)(2,1)S(1)} %all_gather.6, bf16[2,3072,512]{2,1,0:T(8,128)(2,1)} %param.10, f32[4,2,16,512]{3,2,0,1:T(8,128)S(1)} %fusion.16), kind=kOutput, calls=%fused_computation.11 | convolution fusion | flops 805699584 | bytes 15204352 | tf_op jit(solution)/shard_map/gesf,efd->gesd/dot_general | solution.py:53
  104.9 0.0 reduce-scatter.5.cloned.1.call-update
  104.9 36.3 %reduce-scatter.5.cloned.1.call-done = f32[4,2,16,384]{3,2,0,1:T(8,128)} async-done(((f32[4,2,16,3072]{3,2,0,1:T(8,128)}), f32[4,2,16,384]{3,2,0,1:T(8,128)}) %reduce-scatter.5.cloned.1.call-update) | async-done | bytes 196624 | tf_op jit(solution)/shard_map/reduce_scatter | solution.py:56
  141.2 0.9 convert_element_type.30
  142.1 0.7 copy.10
  142.8 4.6 %all-to-all-start.1 = ((bf16[4,2,16,384]{3,2,1,0:T(8,128)(2,1)}), bf16[4,2,16,384]{3,2,1,0:T(8,128)(2,1)S(1)}, u32[]{:S(2)}, u32[]{:S(2)}) async-start(bf16[4,2,16,384]{3,2,1,0:T(8,128)(2,1)} %copy.10), calls=%async_computation.3 | async-start | bytes 196608 | tf_op jit(solution)/shard_map/all_to_all | solution.py:59
  147.4 0.3 divide_convert_fusion
  147.7 5.5 %all-to-all-done.1 = bf16[4,2,16,384]{3,2,1,0:T(8,128)(2,1)S(1)} async-done(((bf16[4,2,16,384]{3,2,1,0:T(8,128)(2,1)}), bf16[4,2,16,384]{3,2,1,0:T(8,128)(2,1)S(1)}, u32[]{:S(2)}, u32[]{:S(2)}) %all-to-all-start.1) | async-done | bytes 98336 | tf_op jit(solution)/shard_map/all_to_all | solution.py:59
  153.2 10.9 %all_gather.7 = bf16[4,2,16,3072]{3,2,1,0:T(8,128)(2,1)S(1)} all-gather(bf16[4,2,16,384]{3,2,1,0:T(8,128)(2,1)S(1)} %all-to-all-done.1), channel_id=1, replica_groups=mesh['seq'=8,'grp'=4] {'seq'}, dimensions={3}, use_global_device_ids=true | all-gather | bytes 884736 | tf_op jit(solution)/shard_map/all_gather | solution.py:63
  164.1 4.5 %convert_bitcast_fusion = bf16[1,1024,3072]{2,1,0:T(8,128)(2,1)} fusion(bf16[1024,128]{1,0:T(8,128)(2,1)S(1)} %divide_convert_fusion, bf16[128,3072]{1,0:T(8,128)(2,1)S(1)} %bitcast.71), kind=kOutput, calls=%fused_computation.10 | convolution fusion | flops 808452096 | bytes 7340032 | tf_op jit(solution)/shard_map/dot_general | solution.py:65
  (3 shorter events, 0.1 us)
Async XLA Ops:
  6.5 1.1 copy-start
  6.5 64.2 %reduce-scatter.3.cloned.1.call-start = ((), (), s32[]{:S(2)}) async-start(), calls=%async_computation.4 | async-start | bytes 1769472 | tf_op jit(solution)/shard_map/reduce_scatter | solution.py:33
  32.8 108.3 %reduce-scatter.5.cloned.1.call-start = ((), (), s32[]{:S(2)}) async-start(), calls=%async_computation.5 | async-start | bytes 1769472 | tf_op jit(solution)/shard_map/reduce_scatter | solution.py:56
  142.8 10.4 %all-to-all-start.1 = ((bf16[4,2,16,384]{3,2,1,0:T(8,128)(2,1)}), bf16[4,2,16,384]{3,2,1,0:T(8,128)(2,1)S(1)}, u32[]{:S(2)}, u32[]{:S(2)}) async-start(bf16[4,2,16,384]{3,2,1,0:T(8,128)(2,1)} %copy.10), calls=%async_computation.3 | async-start | bytes 196608 | tf_op jit(solution)/shard_map/all_to_all | solution.py:59
Sparse Core Ops, SparseCore 0:
  33.0 37.6 reduce-scatter.2
  105.0 36.0 reduce-scatter.4
where the time goes:
time: 176 us; the launch traced here: 175 us
  waiting for transfers between devices  67.8 us (39%)
  blocking collectives  59 us (34%)
  matrix products  26.1 us (15%)
  between operations  13.4 us (8%)
  starting transfers between devices  4.63 us (3%)
  other arithmetic  3.46 us (2%)
    reduce_scatter x1, waiting for transfers between devices, body(): lax.psum_scatter(partial_value, 'seq', scatter_dimension=3, tiled=True)  36.3 us
    reduce_scatter x1, waiting for transfers between devices, body(): lax.psum_scatter(rows_loc, 'seq', scatter_dimension=1, tiled=True)  26 us
    pmax x1, blocking collectives, body(): global_peak = lax.pmax(local_peak, 'seq')  15.2 us
    psum x1, blocking collectives, body(): totals = lax.psum(totals_loc, 'seq')  11.8 us
    all_gather x1, blocking collectives, body(): columns_in = lax.all_gather(arrived, 'seq', axis=3, tiled=True)  10.9 us
    all_gather x1, blocking collectives, body(): columns_in = lax.all_gather(returned, 'seq', axis=3, tiled=True)  10.9 us
    all_to_all x1, blocking collectives, body(): lax.all_to_all(slot_part.reshape(groups, slot_count // groups, col_width)...  10.2 us
    dot_general x1, matrix products, body(): jnp.einsum('gesf,efd->gesd', hidden, down_weight, preferred_element_type=...  8.05 us
  transfers between devices with their start and end apart: 3, of which 3 were waited for; matrix products, arithmetic and copies ran while one was open for 0% of the time, Pallas kernels for 0%

commit v1 on v0

v1 whole, which is shorter than its diff:
```python
import jax
import jax.numpy as jnp
from jax import lax
from jax.experimental import pallas as pl
from jax.experimental.pallas import tpu as pltpu
from jax.sharding import PartitionSpec as P

BLOCK = 128
LANES = 128
FLOOR = -1e30
F32 = jnp.float32
BF16 = jnp.bfloat16


def pack_stats(peak, total):
    rows = peak.shape[0]
    lane = lax.broadcasted_iota(jnp.int32, (rows, LANES), 1)
    block = jnp.zeros((rows, LANES), BF16).astype(F32)
    at = 0
    for value in (peak, total):
        rest = jnp.broadcast_to(value, (rows, LANES))
        for _ in range(3):
            part = rest.astype(BF16).astype(F32)
            block = jnp.where(lane == at, part, block)
            rest = rest - part
            at += 1
    return block.astype(BF16)


def unpack_stats(block):
    block = block.astype(F32)
    lane = lax.broadcasted_iota(jnp.int32, block.shape, 1)
    peak = jnp.sum(jnp.where(lane < 3, block, 0.0), axis=1, keepdims=True)
    total = jnp.sum(jnp.where((lane >= 3) & (lane < 6), block, 0.0), axis=1, keepdims=True)
    return peak, total


def merge(refs, rows, width):
    stats = [unpack_stats(ref[rows, width:]) for ref in refs]
    peak = stats[0][0]
    for other, _ in stats[1:]:
        peak = jnp.maximum(peak, other)
    scales = [jnp.exp(own - peak) for own, _ in stats]
    total = sum(s * t for s, (_, t) in zip(scales, stats))
    summed = sum(s * ref[rows, :width].astype(F32) for s, ref in zip(scales, refs))
    return peak, total, summed


def body_for(mesh):
    n_seq, n_grp = mesh.shape["seq"], mesh.shape["grp"]
    major = 1
    while major * major < n_seq:
        major *= 2
    minor = n_seq // major
    total_devices = n_seq * n_grp
    assert major * minor == n_seq and n_grp & (n_grp - 1) == 0

    def exchange(x, step, unit):
        pairs = []
        for i in range(total_devices):
            s, g = divmod(i, n_grp)
            if unit == "minor":
                s ^= step
            elif unit == "major":
                s ^= step * minor
            else:
                g ^= step
            pairs.append((i, s * n_grp + g))
        return lax.ppermute(x, ("seq", "grp"), pairs)

    def body(tokens, block_map, slot_keys, gate_weight, up_weight, down_weight):
        rows_here, width_all = tokens.shape[1:]
        slots = slot_keys.shape[1]
        blocks = block_map.shape[1]
        exp_dev, _, ff = gate_weight.shape
        width = width_all // minor
        wide = width + LANES
        piece = slots // major
        grain = piece // n_grp
        per_grp = slots // n_grp
        image_slots = 3 * slots // 4
        per_exp = major // exp_dev
        chunks = 4
        step_rows = rows_here // chunks
        blocks_in = blocks // chunks
        any_spec = pl.BlockSpec(memory_space=pl.ANY)
        vmem_spec = pl.BlockSpec(memory_space=pltpu.VMEM)
        smem_spec = pl.BlockSpec(memory_space=pltpu.SMEM)

        def place():
            s = lax.axis_index("seq")
            return s // minor, s % minor, lax.axis_index("grp")

        def shape(*dims):
            return jax.ShapeDtypeStruct(dims, BF16)

        def slot_ids(dims, dim):
            k, _, z = place()
            at = lax.broadcasted_iota(jnp.int32, dims, dim)
            p = at // piece
            q = (at % piece) // grain
            r = at % grain
            return (z ^ q) * per_grp + (k ^ p) * grain + r

        def column(off, size):
            return pl.ds(pl.multiple_of(off, LANES), size)

        def dispatch(tok_hbm, map_ref, keys_ref, *refs):
            outs = refs[:minor]
            mix_ref, tok, keys_p, logit, wt, sems = refs[minor:]
            k, m, z = place()
            copies = []
            for c in range(chunks):
                for h in range(minor):
                    cp = pltpu.make_async_copy(
                        tok_hbm.at[0, pl.ds(c * step_rows, step_rows), column((m ^ h) * width, width)],
                        tok.at[h, pl.ds(c * step_rows, step_rows), :],
                        sems.at[c, h],
                    )
                    cp.start()
                    copies.append(cp)
            wanted = slot_ids((slots, slots), 1)
            chosen = (lax.broadcasted_iota(jnp.int32, (slots, slots), 0) == wanted).astype(F32).astype(BF16)
            for h in range(minor):
                keys_p[h] = jnp.dot(
                    keys_ref[pl.ds((m ^ h) * width, width), :], chosen, preferred_element_type=F32
                ).astype(BF16)
            text = (slot_ids((1, slots), 1) >= image_slots).astype(jnp.int32)
            peak = jnp.full((1, slots), FLOOR, F32)
            for c in range(chunks):
                rows = slice(c * step_rows, (c + 1) * step_rows)
                value = None
                for h in range(minor):
                    copies[c * minor + h].wait()
                    part = jnp.dot(tok[h, rows, :], keys_p[h], preferred_element_type=F32)
                    value = part if value is None else value + part
                for b in range(blocks_in):
                    at = c * blocks_in + b
                    rows_b = slice(at * BLOCK, (at + 1) * BLOCK)
                    allowed = text == map_ref[0, at]
                    masked = jnp.where(allowed, value[b * BLOCK : (b + 1) * BLOCK], FLOOR)
                    logit[rows_b, :] = masked
                    peak = jnp.maximum(peak, jnp.max(masked, axis=0, keepdims=True))
                    row_peak = jnp.max(masked, axis=1, keepdims=True)
                    score = jnp.where(allowed, jnp.exp(masked - row_peak), 0.0)
                    mix_ref[rows_b, :] = (score / jnp.sum(score, axis=1, keepdims=True)).astype(BF16)
            total = jnp.zeros((1, slots), F32)
            for at in range(blocks):
                rows_b = slice(at * BLOCK, (at + 1) * BLOCK)
                allowed = text == map_ref[0, at]
                weight = jnp.where(allowed, jnp.exp(logit[rows_b, :] - peak), 0.0)
                total = total + jnp.sum(weight, axis=0, keepdims=True)
                wt[:, rows_b] = weight.T.astype(BF16)
            stats = pack_stats(
                jnp.broadcast_to(peak, (slots, slots)).T[:, :1],
                jnp.broadcast_to(total, (slots, slots)).T[:, :1],
            )
            for h in reversed(range(minor)):
                outs[h][:, width:] = stats
                outs[h][:, :width] = jnp.dot(wt[...], tok[h], preferred_element_type=F32).astype(BF16)

        *parts, mix = pl.pallas_call(
            dispatch,
            name="dispatch",
            in_specs=[any_spec, smem_spec, vmem_spec],
            out_specs=[vmem_spec] * (minor + 1),
            out_shape=[shape(slots, wide)] * minor + [shape(rows_here, slots)],
            scratch_shapes=[
                pltpu.VMEM((minor, rows_here, width), BF16),
                pltpu.VMEM((minor, width, slots), BF16),
                pltpu.VMEM((rows_here, slots), F32),
                pltpu.VMEM((slots, rows_here), BF16),
                pltpu.SemaphoreType.DMA((chunks, minor)),
            ],
        )(tokens, block_map, slot_keys)

        parts = [parts[0]] + [exchange(parts[h], h, "minor") for h in range(1, minor)]

        def merge_minor(*refs):
            ins, outs = refs[:minor], refs[minor:]
            for p in range(major):
                peak, total, summed = merge(ins, slice(p * piece, (p + 1) * piece), width)
                outs[p][:, :width] = summed.astype(BF16)
                outs[p][:, width:] = pack_stats(peak, total)

        parts = pl.pallas_call(
            merge_minor,
            name="merge_minor",
            in_specs=[vmem_spec] * minor,
            out_specs=[vmem_spec] * major,
            out_shape=[shape(piece, wide)] * major,
        )(*parts)

        parts = [parts[0]] + [exchange(parts[p], p, "major") for p in range(1, major)]

        def merge_major(*refs):
            ins, outs = refs[:major], refs[major:]
            _, total, summed = merge(ins, slice(None), width)
            value = summed / total
            for q in range(n_grp):
                outs[q][...] = value[q * grain : (q + 1) * grain].astype(BF16)

        parts = pl.pallas_call(
            merge_major,
            name="merge_major",
            in_specs=[vmem_spec] * major,
            out_specs=[vmem_spec] * n_grp,
            out_shape=[shape(grain, width)] * n_grp,
        )(*parts)

        def spread(parts):
            parts = [parts[0]] + [exchange(parts[q], q, "grp") for q in range(1, n_grp)]
            whole = jnp.concatenate(parts, axis=0)
            whole = [whole] + [exchange(whole, p, "major") for p in range(1, major)]
            return [whole] + [[exchange(x, h, "minor") for x in whole] for h in range(1, minor)]

        gathered = spread(parts)

        def experts(*refs):
            ins = refs[: minor * major]
            gate_hbm, up_hbm, down_hbm = refs[minor * major : minor * major + 3]
            outs = refs[minor * major + 3 : minor * major + 3 + minor]
            gate_v, up_v, down_v, sems = refs[minor * major + 3 + minor :]
            k, m, _ = place()
            copies = {}
            for t in range(exp_dev):
                e = (k // per_exp) ^ t
                for h in range(minor):
                    rows = pl.ds(pl.multiple_of((m ^ h) * width, LANES), width)
                    for i, (src, dst) in enumerate(((gate_hbm, gate_v), (up_hbm, up_v))):
                        cp = pltpu.make_async_copy(src.at[e, rows, :], dst.at[t, h], sems.at[i, t, h])
                        cp.start()
                        copies[i, t, h] = cp
                for h in range(minor):
                    cp = pltpu.make_async_copy(
                        down_hbm.at[e, :, column((m ^ h) * width, width)], down_v.at[t, h], sems.at[2, t, h]
                    )
                    cp.start()
                    copies[2, t, h] = cp
            for t in range(exp_dev):
                gate = up = None
                for h in range(minor):
                    x = jnp.concatenate(
                        [ins[h * major + p][...] for p in range(t * per_exp, (t + 1) * per_exp)], axis=0
                    )
                    copies[0, t, h].wait()
                    g = jnp.dot(x, gate_v[t, h], preferred_element_type=F32)
                    gate = g if gate is None else gate + g
                    copies[1, t, h].wait()
                    u = jnp.dot(x, up_v[t, h], preferred_element_type=F32)
                    up = u if up is None else up + u
                hidden = (gate / (1.0 + jnp.exp(-gate)) * up).astype(BF16)
                rows = slice(t * per_exp * piece, (t + 1) * per_exp * piece)
                for h in range(minor):
                    copies[2, t, h].wait()
                    outs[h][rows, :] = jnp.dot(hidden, down_v[t, h], preferred_element_type=F32).astype(BF16)

        parts = pl.pallas_call(
            experts,
            name="experts",
            in_specs=[vmem_spec] * (minor * major) + [any_spec] * 3,
            out_specs=[vmem_spec] * minor,
            out_shape=[shape(major * piece, width)] * minor,
            scratch_shapes=[
                pltpu.VMEM((exp_dev, minor, width, ff), BF16),
                pltpu.VMEM((exp_dev, minor, width, ff), BF16),
                pltpu.VMEM((exp_dev, minor, ff, width), BF16),
                pltpu.SemaphoreType.DMA((3, exp_dev, minor)),
            ],
        )(*[x for group in gathered for x in group], gate_weight, up_weight, down_weight)

        parts = [parts[0]] + [exchange(parts[h], h, "minor") for h in range(1, minor)]

        def add_minor(*refs):
            ins, outs = refs[:minor], refs[minor:]
            for p in range(major):
                rows = slice(p * piece, (p + 1) * piece)
                outs[p][...] = sum(ref[rows, :].astype(F32) for ref in ins).astype(BF16)

        parts = pl.pallas_call(
            add_minor,
            name="add_minor",
            in_specs=[vmem_spec] * minor,
            out_specs=[vmem_spec] * major,
            out_shape=[shape(piece, width)] * major,
        )(*parts)

        parts = [parts[0]] + [exchange(parts[p], p, "major") for p in range(1, major)]

        def add_major(*refs):
            ins, outs = refs[:major], refs[major:]
            value = sum(ref[...].astype(F32) for ref in ins)
            for q in range(n_grp):
                outs[q][...] = value[q * grain : (q + 1) * grain].astype(BF16)

        parts = pl.pallas_call(
            add_major,
            name="add_major",
            in_specs=[vmem_spec] * major,
            out_specs=[vmem_spec] * n_grp,
            out_shape=[shape(grain, width)] * n_grp,
        )(*parts)

        gathered = spread(parts)

        def combine(mix_ref, *refs):
            ins = refs[: minor * major]
            out_hbm, stage, sems = refs[minor * major :]
            _, m, _ = place()
            copies = []
            for c in range(chunks):
                rows = slice(c * step_rows, (c + 1) * step_rows)
                for h in range(minor):
                    value = jnp.concatenate([ins[h * major + p][...] for p in range(major)], axis=0)
                    stage[h, rows, :] = jnp.dot(
                        mix_ref[rows, :], value, preferred_element_type=F32
                    ).astype(BF16)
                    cp = pltpu.make_async_copy(
                        stage.at[h, rows, :],
                        out_hbm.at[0, rows, column((m ^ h) * width, width)],
                        sems.at[c, h],
                    )
                    cp.start()
                    copies.append(cp)
            for cp in copies:
                cp.wait()

        return pl.pallas_call(
            combine,
            name="combine",
            in_specs=[vmem_spec] * (1 + minor * major),
            out_specs=any_spec,
            out_shape=shape(1, rows_here, width_all),
            scratch_shapes=[
                pltpu.VMEM((minor, rows_here, width), BF16),
                pltpu.SemaphoreType.DMA((chunks, minor)),
            ],
        )(mix, *[x for group in gathered for x in group])

    return body


def solution(mesh):
    placed = (
        P("grp", "seq", None),
        P("grp", "seq"),
        P(),
        P("grp", None, "seq"),
        P("grp", None, "seq"),
        P("grp", "seq", None),
    )
    return jax.shard_map(
        body_for(mesh), mesh=mesh, in_specs=placed, out_specs=P("grp", "seq", None), check_vma=False
    )
```

time: 176 us -> 89.4 us (0.51)
  blocking collectives: 59 us -> 0 us
  waiting for transfers between devices: 67.8 us -> 30.1 us
  Pallas kernels: 0 us -> 28.7 us
  matrix products: 26.1 us -> 0 us
  starting transfers between devices: 4.63 us -> 24.4 us
  between operations: 13.4 us -> 0.2 us
  local copies, waits for them, and re-layouts: 1 us -> 5.54 us
  other arithmetic: 3.46 us -> 0 us
    reduce_scatter x2 -> x0, waiting for transfers between devices: 62.3 us -> none  [the longest x1 36.3 us: body(): lax.psum_scatter(partial_value, 'seq', scatter_dimension=3, tiled=True)]
    ppermute x0 -> x28, waiting for transfers between devices: none -> 30.1 us  [exchange(): return lax.ppermute(x, ('seq', 'grp'), pairs)]
    pallas_call x0 -> x7, Pallas kernels: none -> 28.7 us  [the longest x1 9.28 us: body(): pl.pallas_call(experts, name='experts', in_specs=[vmem_spec] * (minor * m...]
    dot_general x5 -> x0, matrix products: 26.1 us -> none  [the longest x1 8.05 us: body(): jnp.einsum('gesf,efd->gesd', hidden, down_weight, preferred_element_type=...]
    ppermute x0 -> x28, starting transfers between devices: none -> 24.4 us  [exchange(): return lax.ppermute(x, ('seq', 'grp'), pairs)]
    all_gather x2 -> x0, blocking collectives: 21.8 us -> none  [the longest x1 10.9 us: body(): columns_in = lax.all_gather(arrived, 'seq', axis=3, tiled=True)]
    pmax x1 -> x0, blocking collectives: 15.2 us -> none  [body(): global_peak = lax.pmax(local_peak, 'seq')]
    psum x1 -> x0, blocking collectives: 11.8 us -> none  [body(): totals = lax.psum(totals_loc, 'seq')]
  transfers between devices with their start and end apart: 3 -> 28, of which waited for: 3 -> 21; matrix products, arithmetic and copies ran while one was open for 0% -> 2% of each run, Pallas kernels for 0% -> 0%
where the time goes in v1:
time: 89.4 us; the launch traced here: 88.9 us
  waiting for transfers between devices  30.1 us (34%)
  Pallas kernels  28.7 us (32%)
  starting transfers between devices  24.4 us (27%)
  local copies, waits for them, and re-layouts  5.54 us (6%)
    ppermute x28, waiting for transfers between devices, exchange(): return lax.ppermute(x, ('seq', 'grp'), pairs)  30.1 us
    ppermute x28, starting transfers between devices, exchange(): return lax.ppermute(x, ('seq', 'grp'), pairs)  24.4 us
    pallas_call x1, Pallas kernels, body(): pl.pallas_call(experts, name='experts', in_specs=[vmem_spec] * (minor * m...  9.28 us
    pallas_call x1, Pallas kernels, body(): pl.pallas_call(dispatch, name='dispatch', in_specs=[any_spec, smem_spec,...  7.54 us
    unnamed x54, local copies, waits for them, and re-layouts  5.53 us
    pallas_call x1, Pallas kernels, body(): pl.pallas_call(combine, name='combine', in_specs=[vmem_spec] * (1 + minor...  4.34 us
    pallas_call x1, Pallas kernels, body(): pl.pallas_call(merge_minor, name='merge_minor', in_specs=[vmem_spec] * mi...  2.13 us
    pallas_call x1, Pallas kernels, body(): pl.pallas_call(add_minor, name='add_minor', in_specs=[vmem_spec] * minor,...  1.91 us
  transfers between devices with their start and end apart: 28, of which 21 were waited for; matrix products, arithmetic and copies ran while one was open for 2% of the time, Pallas kernels for 0%

profile of v1, /device:TPU:0, one launch (start us, length us, event | category | flops | bytes accessed | tf_op | source)
XLA Modules:
  0.0 88.9 jit_solution(15442325303330882968)
XLA Ops:
  0.0 7.5 %dispatch.1 = (bf16[128,1664]{1,0:T(8,128)(2,1)}, bf16[128,1664]{1,0:T(8,128)(2,1)}, bf16[1024,128]{1,0:T(8,128)(2,1)}) custom-call(bf16[1,1024,3072]{2,1,0:T(8,128)(2,1)} %tok_hbm.1, s32[1,8]{1,0:T(1,128)} %map_ref.1, bf16[3072,128]{1,0:T(8,128)(2,1)} %keys_ref.1), custom_call_target="tpu_custom_call" | custom-call | tf_op jit(solution)/shard_map/dispatch/pallas_call | solution.py:162
  8.1 1.6 %collective-permute-done.refs_1_ = bf16[128,1664]{1,0:T(8,128)(2,1)S(1)} collective-permute-done((bf16[128,1664]{1,0:T(8,128)(2,1)}, bf16[128,1664]{1,0:T(8,128)(2,1)S(1)}, u32[]{:S(2)}, u32[]{:S(2)}) %collective-permute-start) | collective-permute-done | bytes 426016 | tf_op jit(solution)/shard_map/ppermute | solution.py:69
  9.7 0.7 copy-done
  10.5 2.1 %merge_minor.1 = (bf16[32,1664]{1,0:T(8,128)(2,1)}, bf16[32,1664]{1,0:T(8,128)(2,1)}, bf16[32,1664]{1,0:T(8,128)(2,1)}, bf16[32,1664]{1,0:T(8,128)(2,1)}) custom-call(bf16[128,1664]{1,0:T(8,128)(2,1)} %get-tuple-element.27.refs_0_, bf16[128,1664]{1,0:T(8,128)(2,1)} %copy-done), custom_call_target="tpu_custom_call" | custom-call | tf_op jit(solution)/shard_map/merge_minor/pallas_call | solution.py:186
  12.6 2.9 %collective-permute-start.1 = (bf16[32,1664]{1,0:T(8,128)(2,1)}, bf16[32,1664]{1,0:T(8,128)(2,1)S(1)}, u32[]{:S(2)}, u32[]{:S(2)}) collective-permute-start(bf16[32,1664]{1,0:T(8,128)(2,1)} %get-tuple-element.30), channel_id=1, source_target_pairs={{0,8},{1,9},{2,10},{3,11},{4,12},{5,13},{6,14},{7,15},{8,0},{9,1},... | collective-permute-start | bytes 319496 | tf_op jit(solution)/shard_map/ppermute | solution.py:69
  15.4 1.5 %collective-permute-start.2 = (bf16[32,1664]{1,0:T(8,128)(2,1)}, bf16[32,1664]{1,0:T(8,128)(2,1)S(1)}, u32[]{:S(2)}, u32[]{:S(2)}) collective-permute-start(bf16[32,1664]{1,0:T(8,128)(2,1)} %get-tuple-element.31), channel_id=1, source_target_pairs={{0,16},{1,17},{2,18},{3,19},{4,20},{5,21},{6,22},{7,23},{8,24},{9,... | collective-permute-start | bytes 319496 | tf_op jit(solution)/shard_map/ppermute | solution.py:69
  17.0 2.2 %collective-permute-done.1.refs_1_ = bf16[32,1664]{1,0:T(8,128)(2,1)S(1)} collective-permute-done((bf16[32,1664]{1,0:T(8,128)(2,1)}, bf16[32,1664]{1,0:T(8,128)(2,1)S(1)}, u32[]{:S(2)}, u32[]{:S(2)}) %collective-permute-start.1) | collective-permute-done | bytes 106528 | tf_op jit(solution)/shard_map/ppermute | solution.py:69
  19.1 2.7 %collective-permute-done.2.refs_2_ = bf16[32,1664]{1,0:T(8,128)(2,1)S(1)} collective-permute-done((bf16[32,1664]{1,0:T(8,128)(2,1)}, bf16[32,1664]{1,0:T(8,128)(2,1)S(1)}, u32[]{:S(2)}, u32[]{:S(2)}) %collective-permute-start.2) | collective-permute-done | bytes 106528 | tf_op jit(solution)/shard_map/ppermute | solution.py:69
  21.8 1.0 %collective-permute-done.3.refs_3_ = bf16[32,1664]{1,0:T(8,128)(2,1)S(1)} collective-permute-done((bf16[32,1664]{1,0:T(8,128)(2,1)}, bf16[32,1664]{1,0:T(8,128)(2,1)S(1)}, u32[]{:S(2)}, u32[]{:S(2)}) %collective-permute-start.3) | collective-permute-done | bytes 106528 | tf_op jit(solution)/shard_map/ppermute | solution.py:69
  22.8 0.6 copy-done.6
  23.4 1.8 %merge_major.1 = (bf16[8,1536]{1,0:T(8,128)(2,1)}, bf16[8,1536]{1,0:T(8,128)(2,1)}, bf16[8,1536]{1,0:T(8,128)(2,1)}, bf16[8,1536]{1,0:T(8,128)(2,1)}) custom-call(bf16[32,1664]{1,0:T(8,128)(2,1)} %get-tuple-element.29.refs_0_, bf16[32,1664]{1,0:T(8,128)(2,1)} %copy-done.4, bf16[32,1664]{1,0:T(8,128)(2,1)} %copy-done.5, bf16[32,1664]{1,0:T(8,128)(2,1)} %copy-done.6), custom_call_target="tpu_custom_call" | custom-call | tf_op jit(solution)/shard_map/merge_major/pallas_call | solution.py:203
  25.3 1.6 %collective-permute-start.4 = (bf16[8,1536]{1,0:T(8,128)(2,1)}, bf16[8,1536]{1,0:T(8,128)(2,1)S(1)}, u32[]{:S(2)}, u32[]{:S(2)}) collective-permute-start(bf16[8,1536]{1,0:T(8,128)(2,1)} %get-tuple-element.34), channel_id=1, source_target_pairs={{0,1},{1,0},{2,3},{3,2},{4,5},{5,4},{6,7},{7,6},{8,9},{9,8},{10,11... | collective-permute-start | bytes 73736 | tf_op jit(solution)/shard_map/ppermute | solution.py:69
  26.8 2.6 %collective-permute-start.5 = (bf16[8,1536]{1,0:T(8,128)(2,1)}, bf16[8,1536]{1,0:T(8,128)(2,1)S(1)}, u32[]{:S(2)}, u32[]{:S(2)}) collective-permute-start(bf16[8,1536]{1,0:T(8,128)(2,1)} %get-tuple-element.35), channel_id=1, source_target_pairs={{0,2},{1,3},{2,0},{3,1},{4,6},{5,7},{6,4},{7,5},{8,10},{9,11},{10,... | collective-permute-start | bytes 73736 | tf_op jit(solution)/shard_map/ppermute | solution.py:69
  29.6 0.7 constant_dynamic-update-slice_fusion.3
  30.4 1.5 %collective-permute-done.5 = bf16[8,1536]{1,0:T(8,128)(2,1)S(1)} collective-permute-done((bf16[8,1536]{1,0:T(8,128)(2,1)}, bf16[8,1536]{1,0:T(8,128)(2,1)S(1)}, u32[]{:S(2)}, u32[]{:S(2)}) %collective-permute-start.5) | collective-permute-done | bytes 24608 | tf_op jit(solution)/shard_map/ppermute | solution.py:69
  31.9 3.3 %collective-permute-done.6 = bf16[8,1536]{1,0:T(8,128)(2,1)S(1)} collective-permute-done((bf16[8,1536]{1,0:T(8,128)(2,1)}, bf16[8,1536]{1,0:T(8,128)(2,1)S(1)}, u32[]{:S(2)}, u32[]{:S(2)}) %collective-permute-start.6) | collective-permute-done | bytes 24608 | tf_op jit(solution)/shard_map/ppermute | solution.py:69
  35.3 1.4 %collective-permute-start.9 = (bf16[32,1536]{1,0:T(8,128)(2,1)S(1)}, bf16[32,1536]{1,0:T(8,128)(2,1)S(1)}, u32[]{:S(2)}, u32[]{:S(2)}) collective-permute-start(bf16[32,1536]{1,0:T(8,128)(2,1)S(1)} %constant_dynamic-update-slice_fusion.refs_0_), channel_id=1, source_target_pairs={{0,24},{1,25},{2,26},{3,27},{4,28},{5,29},{6,30},{7,31},{8,16},{9,... | collective-permute-start | bytes 294920 | tf_op jit(solution)/shard_map/ppermute | solution.py:69
  36.7 1.2 %collective-permute-start.8 = (bf16[32,1536]{1,0:T(8,128)(2,1)S(1)}, bf16[32,1536]{1,0:T(8,128)(2,1)S(1)}, u32[]{:S(2)}, u32[]{:S(2)}) collective-permute-start(bf16[32,1536]{1,0:T(8,128)(2,1)S(1)} %constant_dynamic-update-slice_fusion.refs_0_), channel_id=1, source_target_pairs={{0,16},{1,17},{2,18},{3,19},{4,20},{5,21},{6,22},{7,23},{8,24},{9,... | collective-permute-start | bytes 294920 | tf_op jit(solution)/shard_map/ppermute | solution.py:69
  37.9 0.9 %collective-permute-start.7 = (bf16[32,1536]{1,0:T(8,128)(2,1)S(1)}, bf16[32,1536]{1,0:T(8,128)(2,1)S(1)}, u32[]{:S(2)}, u32[]{:S(2)}) collective-permute-start(bf16[32,1536]{1,0:T(8,128)(2,1)S(1)} %constant_dynamic-update-slice_fusion.refs_0_), channel_id=1, source_target_pairs={{0,8},{1,9},{2,10},{3,11},{4,12},{5,13},{6,14},{7,15},{8,0},{9,1},... | collective-permute-start | bytes 294920 | tf_op jit(solution)/shard_map/ppermute | solution.py:69
  38.8 2.1 %collective-permute-done.9.refs_3_ = bf16[32,1536]{1,0:T(8,128)(2,1)S(1)} collective-permute-done((bf16[32,1536]{1,0:T(8,128)(2,1)S(1)}, bf16[32,1536]{1,0:T(8,128)(2,1)S(1)}, u32[]{:S(2)}, u32[]{:S(2)}) %collective-permute-start.9) | collective-permute-done | bytes 98336 | tf_op jit(solution)/shard_map/ppermute | solution.py:69
  40.8 1.0 %collective-permute-done.8.refs_2_ = bf16[32,1536]{1,0:T(8,128)(2,1)S(1)} collective-permute-done((bf16[32,1536]{1,0:T(8,128)(2,1)S(1)}, bf16[32,1536]{1,0:T(8,128)(2,1)S(1)}, u32[]{:S(2)}, u32[]{:S(2)}) %collective-permute-start.8) | collective-permute-done | bytes 98336 | tf_op jit(solution)/shard_map/ppermute | solution.py:69
  41.8 0.6 collective-permute-done.7.refs_1_
  42.5 0.6 collective-permute-done.12.refs_6_
  43.1 0.6 collective-permute-done.11.refs_5_
  43.8 0.6 copy-done.19
  44.5 9.3 %experts.1 = (bf16[128,1536]{1,0:T(8,128)(2,1)}, bf16[128,1536]{1,0:T(8,128)(2,1)}) custom-call(bf16[32,1536]{1,0:T(8,128)(2,1)} %copy-done.2, bf16[32,1536]{1,0:T(8,128)(2,1)} %copy-done.11, bf16[32,1536]{1,0:T(8,128)(2,1)} %copy-done.9, bf16[32,1536]{1,0:T(8,128)(2,1)} %copy-done.7, bf16[32,1536]{1,0:T(8,128)(2,1)} %copy-done.13, ...), custom_call_target="tpu_custom_call" | custom-call | tf_op jit(solution)/shard_map/experts/pallas_call | solution.py:258
  54.0 1.8 %collective-permute-done.14.refs_1_ = bf16[128,1536]{1,0:T(8,128)(2,1)S(1)} collective-permute-done((bf16[128,1536]{1,0:T(8,128)(2,1)}, bf16[128,1536]{1,0:T(8,128)(2,1)S(1)}, u32[]{:S(2)}, u32[]{:S(2)}) %collective-permute-start.14) | collective-permute-done | bytes 393248 | tf_op jit(solution)/shard_map/ppermute | solution.py:69
  55.8 0.7 copy-done.1
  56.5 1.9 %add_minor.1 = (bf16[32,1536]{1,0:T(8,128)(2,1)}, bf16[32,1536]{1,0:T(8,128)(2,1)}, bf16[32,1536]{1,0:T(8,128)(2,1)}, bf16[32,1536]{1,0:T(8,128)(2,1)}) custom-call(bf16[128,1536]{1,0:T(8,128)(2,1)} %get-tuple-element.37.refs_0_, bf16[128,1536]{1,0:T(8,128)(2,1)} %copy-done.1), custom_call_target="tpu_custom_call" | custom-call | tf_op jit(solution)/shard_map/add_minor/pallas_call | solution.py:280
  58.4 1.1 %collective-permute-start.15 = (bf16[32,1536]{1,0:T(8,128)(2,1)}, bf16[32,1536]{1,0:T(8,128)(2,1)S(1)}, u32[]{:S(2)}, u32[]{:S(2)}) collective-permute-start(bf16[32,1536]{1,0:T(8,128)(2,1)} %get-tuple-element.40), channel_id=1, source_target_pairs={{0,8},{1,9},{2,10},{3,11},{4,12},{5,13},{6,14},{7,15},{8,0},{9,1},... | collective-permute-start | bytes 294920 | tf_op jit(solution)/shard_map/ppermute | solution.py:69
  59.5 1.3 %collective-permute-start.16 = (bf16[32,1536]{1,0:T(8,128)(2,1)}, bf16[32,1536]{1,0:T(8,128)(2,1)S(1)}, u32[]{:S(2)}, u32[]{:S(2)}) collective-permute-start(bf16[32,1536]{1,0:T(8,128)(2,1)} %get-tuple-element.41), channel_id=1, source_target_pairs={{0,16},{1,17},{2,18},{3,19},{4,20},{5,21},{6,22},{7,23},{8,24},{9,... | collective-permute-start | bytes 294920 | tf_op jit(solution)/shard_map/ppermute | solution.py:69
  60.8 1.1 %collective-permute-start.17 = (bf16[32,1536]{1,0:T(8,128)(2,1)}, bf16[32,1536]{1,0:T(8,128)(2,1)S(1)}, u32[]{:S(2)}, u32[]{:S(2)}) collective-permute-start(bf16[32,1536]{1,0:T(8,128)(2,1)} %get-tuple-element.42), channel_id=1, source_target_pairs={{0,24},{1,25},{2,26},{3,27},{4,28},{5,29},{6,30},{7,31},{8,16},{9,... | collective-permute-start | bytes 294920 | tf_op jit(solution)/shard_map/ppermute | solution.py:69
  61.9 1.7 %collective-permute-done.15.refs_1_ = bf16[32,1536]{1,0:T(8,128)(2,1)S(1)} collective-permute-done((bf16[32,1536]{1,0:T(8,128)(2,1)}, bf16[32,1536]{1,0:T(8,128)(2,1)S(1)}, u32[]{:S(2)}, u32[]{:S(2)}) %collective-permute-start.15) | collective-permute-done | bytes 98336 | tf_op jit(solution)/shard_map/ppermute | solution.py:69
  63.6 1.8 %collective-permute-done.16.refs_2_ = bf16[32,1536]{1,0:T(8,128)(2,1)S(1)} collective-permute-done((bf16[32,1536]{1,0:T(8,128)(2,1)}, bf16[32,1536]{1,0:T(8,128)(2,1)S(1)}, u32[]{:S(2)}, u32[]{:S(2)}) %collective-permute-start.16) | collective-permute-done | bytes 98336 | tf_op jit(solution)/shard_map/ppermute | solution.py:69
  65.4 1.1 %collective-permute-done.17.refs_3_ = bf16[32,1536]{1,0:T(8,128)(2,1)S(1)} collective-permute-done((bf16[32,1536]{1,0:T(8,128)(2,1)}, bf16[32,1536]{1,0:T(8,128)(2,1)S(1)}, u32[]{:S(2)}, u32[]{:S(2)}) %collective-permute-start.17) | collective-permute-done | bytes 98336 | tf_op jit(solution)/shard_map/ppermute | solution.py:69
  66.5 0.6 copy-done.23
  67.1 1.7 %add_major.1 = (bf16[8,1536]{1,0:T(8,128)(2,1)}, bf16[8,1536]{1,0:T(8,128)(2,1)}, bf16[8,1536]{1,0:T(8,128)(2,1)}, bf16[8,1536]{1,0:T(8,128)(2,1)}) custom-call(bf16[32,1536]{1,0:T(8,128)(2,1)} %get-tuple-element.39.refs_0_, bf16[32,1536]{1,0:T(8,128)(2,1)} %copy-done.21, bf16[32,1536]{1,0:T(8,128)(2,1)} %copy-done.22, bf16[32,1536]{1,0:T(8,128)(2,1)} %copy-done.23), custom_call_target="tpu_custom_call" | custom-call | tf_op jit(solution)/shard_map/add_major/pallas_call | solution.py:296
  68.8 0.8 collective-permute-start.19
  69.7 3.6 %collective-permute-start.20 = (bf16[8,1536]{1,0:T(8,128)(2,1)}, bf16[8,1536]{1,0:T(8,128)(2,1)S(1)}, u32[]{:S(2)}, u32[]{:S(2)}) collective-permute-start(bf16[8,1536]{1,0:T(8,128)(2,1)} %get-tuple-element.46), channel_id=1, source_target_pairs={{0,3},{1,2},{2,1},{3,0},{4,7},{5,6},{6,5},{7,4},{8,11},{9,10},{10,... | collective-permute-start | bytes 73736 | tf_op jit(solution)/shard_map/ppermute | solution.py:69
  73.2 0.7 constant_dynamic-update-slice_fusion.7
  74.0 1.5 %collective-permute-done.20 = bf16[8,1536]{1,0:T(8,128)(2,1)S(1)} collective-permute-done((bf16[8,1536]{1,0:T(8,128)(2,1)}, bf16[8,1536]{1,0:T(8,128)(2,1)S(1)}, u32[]{:S(2)}, u32[]{:S(2)}) %collective-permute-start.20) | collective-permute-done | bytes 24608 | tf_op jit(solution)/shard_map/ppermute | solution.py:69
  75.5 1.8 %collective-permute-start.23 = (bf16[32,1536]{1,0:T(8,128)(2,1)S(1)}, bf16[32,1536]{1,0:T(8,128)(2,1)S(1)}, u32[]{:S(2)}, u32[]{:S(2)}) collective-permute-start(bf16[32,1536]{1,0:T(8,128)(2,1)S(1)} %constant_dynamic-update-slice_fusion.4.refs_0_), channel_id=1, source_target_pairs={{0,24},{1,25},{2,26},{3,27},{4,28},{5,29},{6,30},{7,31},{8,16},{9,... | collective-permute-start | bytes 294920 | tf_op jit(solution)/shard_map/ppermute | solution.py:69
  77.3 0.8 collective-permute-start.22
  78.0 1.0 %collective-permute-start.21 = (bf16[32,1536]{1,0:T(8,128)(2,1)S(1)}, bf16[32,1536]{1,0:T(8,128)(2,1)S(1)}, u32[]{:S(2)}, u32[]{:S(2)}) collective-permute-start(bf16[32,1536]{1,0:T(8,128)(2,1)S(1)} %constant_dynamic-update-slice_fusion.4.refs_0_), channel_id=1, source_target_pairs={{0,8},{1,9},{2,10},{3,11},{4,12},{5,13},{6,14},{7,15},{8,0},{9,1},... | collective-permute-start | bytes 294920 | tf_op jit(solution)/shard_map/ppermute | solution.py:69
  79.0 2.0 %collective-permute-done.23.refs_3_ = bf16[32,1536]{1,0:T(8,128)(2,1)S(1)} collective-permute-done((bf16[32,1536]{1,0:T(8,128)(2,1)S(1)}, bf16[32,1536]{1,0:T(8,128)(2,1)S(1)}, u32[]{:S(2)}, u32[]{:S(2)}) %collective-permute-start.23) | collective-permute-done | bytes 98336 | tf_op jit(solution)/shard_map/ppermute | solution.py:69
  81.0 1.0 %collective-permute-done.22.refs_2_ = bf16[32,1536]{1,0:T(8,128)(2,1)S(1)} collective-permute-done((bf16[32,1536]{1,0:T(8,128)(2,1)S(1)}, bf16[32,1536]{1,0:T(8,128)(2,1)S(1)}, u32[]{:S(2)}, u32[]{:S(2)}) %collective-permute-start.22) | collective-permute-done | bytes 98336 | tf_op jit(solution)/shard_map/ppermute | solution.py:69
  82.7 0.7 collective-permute-done.26.refs_6_
  84.6 4.3 %combine.1 = bf16[1,1024,3072]{2,1,0:T(8,128)(2,1)} custom-call(bf16[1024,128]{1,0:T(8,128)(2,1)} %get-tuple-element.26.mix_ref, bf16[32,1536]{1,0:T(8,128)(2,1)} %copy-done.3, bf16[32,1536]{1,0:T(8,128)(2,1)} %copy-done.12, bf16[32,1536]{1,0:T(8,128)(2,1)} %copy-done.10, bf16[32,1536]{1,0:T(8,128)(2,1)} %copy-done.8, bf16[32,1536]{1,0:T(8,128)(2,1)} %copy-done.14, ...), custom_call_target="tpu_custom_call" | custom-call | tf_op jit(solution)/shard_map/combine/pallas_call | solution.py:328
  (71 shorter events, 2.9 us)
Async XLA Ops:
  7.5 2.2 %collective-permute-start = (bf16[128,1664]{1,0:T(8,128)(2,1)}, bf16[128,1664]{1,0:T(8,128)(2,1)S(1)}, u32[]{:S(2)}, u32[]{:S(2)}) collective-permute-start(bf16[128,1664]{1,0:T(8,128)(2,1)} %get-tuple-element.28), channel_id=1, source_target_pairs={{0,4},{1,5},{2,6},{3,7},{4,0},{5,1},{6,2},{7,3},{8,12},{9,13},{10,... | collective-permute-start | bytes 1277960 | tf_op jit(solution)/shard_map/ppermute | solution.py:69
  9.7 0.7 copy-start
  12.6 6.5 %collective-permute-start.1 = (bf16[32,1664]{1,0:T(8,128)(2,1)}, bf16[32,1664]{1,0:T(8,128)(2,1)S(1)}, u32[]{:S(2)}, u32[]{:S(2)}) collective-permute-start(bf16[32,1664]{1,0:T(8,128)(2,1)} %get-tuple-element.30), channel_id=1, source_target_pairs={{0,8},{1,9},{2,10},{3,11},{4,12},{5,13},{6,14},{7,15},{8,0},{9,1},... | collective-permute-start | bytes 319496 | tf_op jit(solution)/shard_map/ppermute | solution.py:69
  15.4 6.4 %collective-permute-start.2 = (bf16[32,1664]{1,0:T(8,128)(2,1)}, bf16[32,1664]{1,0:T(8,128)(2,1)S(1)}, u32[]{:S(2)}, u32[]{:S(2)}) collective-permute-start(bf16[32,1664]{1,0:T(8,128)(2,1)} %get-tuple-element.31), channel_id=1, source_target_pairs={{0,16},{1,17},{2,18},{3,19},{4,20},{5,21},{6,22},{7,23},{8,24},{9,... | collective-permute-start | bytes 319496 | tf_op jit(solution)/shard_map/ppermute | solution.py:69
  16.9 5.8 %collective-permute-start.3 = (bf16[32,1664]{1,0:T(8,128)(2,1)}, bf16[32,1664]{1,0:T(8,128)(2,1)S(1)}, u32[]{:S(2)}, u32[]{:S(2)}) collective-permute-start(bf16[32,1664]{1,0:T(8,128)(2,1)} %get-tuple-element.32), channel_id=1, source_target_pairs={{0,24},{1,25},{2,26},{3,27},{4,28},{5,29},{6,30},{7,31},{8,16},{9,... | collective-permute-start | bytes 319496 | tf_op jit(solution)/shard_map/ppermute | solution.py:69
  19.1 3.7 %copy-start.4 = (bf16[32,1664]{1,0:T(8,128)(2,1)}, bf16[32,1664]{1,0:T(8,128)(2,1)S(1)}, u32[]{:S(2)}) copy-start(bf16[32,1664]{1,0:T(8,128)(2,1)S(1)} %collective-permute-done.1.refs_1_) | copy-start | bytes 319492
  21.8 1.0 %copy-start.5 = (bf16[32,1664]{1,0:T(8,128)(2,1)}, bf16[32,1664]{1,0:T(8,128)(2,1)S(1)}, u32[]{:S(2)}) copy-start(bf16[32,1664]{1,0:T(8,128)(2,1)S(1)} %collective-permute-done.2.refs_2_) | copy-start | bytes 319492
  25.3 5.1 %collective-permute-start.4 = (bf16[8,1536]{1,0:T(8,128)(2,1)}, bf16[8,1536]{1,0:T(8,128)(2,1)S(1)}, u32[]{:S(2)}, u32[]{:S(2)}) collective-permute-start(bf16[8,1536]{1,0:T(8,128)(2,1)} %get-tuple-element.34), channel_id=1, source_target_pairs={{0,1},{1,0},{2,3},{3,2},{4,5},{5,4},{6,7},{7,6},{8,9},{9,8},{10,11... | collective-permute-start | bytes 73736 | tf_op jit(solution)/shard_map/ppermute | solution.py:69
  26.8 5.1 %collective-permute-start.5 = (bf16[8,1536]{1,0:T(8,128)(2,1)}, bf16[8,1536]{1,0:T(8,128)(2,1)S(1)}, u32[]{:S(2)}, u32[]{:S(2)}) collective-permute-start(bf16[8,1536]{1,0:T(8,128)(2,1)} %get-tuple-element.35), channel_id=1, source_target_pairs={{0,2},{1,3},{2,0},{3,1},{4,6},{5,7},{6,4},{7,5},{8,10},{9,11},{10,... | collective-permute-start | bytes 73736 | tf_op jit(solution)/shard_map/ppermute | solution.py:69
  29.4 5.8 %collective-permute-start.6 = (bf16[8,1536]{1,0:T(8,128)(2,1)}, bf16[8,1536]{1,0:T(8,128)(2,1)S(1)}, u32[]{:S(2)}, u32[]{:S(2)}) collective-permute-start(bf16[8,1536]{1,0:T(8,128)(2,1)} %get-tuple-element.36), channel_id=1, source_target_pairs={{0,3},{1,2},{2,1},{3,0},{4,7},{5,6},{6,5},{7,4},{8,11},{9,10},{10,... | collective-permute-start | bytes 73736 | tf_op jit(solution)/shard_map/ppermute | solution.py:69
  35.3 8.5 %copy-start.2 = (bf16[32,1536]{1,0:T(8,128)(2,1)}, bf16[32,1536]{1,0:T(8,128)(2,1)S(1)}, u32[]{:S(2)}) copy-start(bf16[32,1536]{1,0:T(8,128)(2,1)S(1)} %constant_dynamic-update-slice_fusion.refs_0_) | copy-start | bytes 294916
  35.3 5.6 %collective-permute-start.9 = (bf16[32,1536]{1,0:T(8,128)(2,1)S(1)}, bf16[32,1536]{1,0:T(8,128)(2,1)S(1)}, u32[]{:S(2)}, u32[]{:S(2)}) collective-permute-start(bf16[32,1536]{1,0:T(8,128)(2,1)S(1)} %constant_dynamic-update-slice_fusion.refs_0_), channel_id=1, source_target_pairs={{0,24},{1,25},{2,26},{3,27},{4,28},{5,29},{6,30},{7,31},{8,16},{9,... | collective-permute-start | bytes 294920 | tf_op jit(solution)/shard_map/ppermute | solution.py:69
  36.7 5.1 %collective-permute-start.8 = (bf16[32,1536]{1,0:T(8,128)(2,1)S(1)}, bf16[32,1536]{1,0:T(8,128)(2,1)S(1)}, u32[]{:S(2)}, u32[]{:S(2)}) collective-permute-start(bf16[32,1536]{1,0:T(8,128)(2,1)S(1)} %constant_dynamic-update-slice_fusion.refs_0_), channel_id=1, source_target_pairs={{0,16},{1,17},{2,18},{3,19},{4,20},{5,21},{6,22},{7,23},{8,24},{9,... | collective-permute-start | bytes 294920 | tf_op jit(solution)/shard_map/ppermute | solution.py:69
  37.9 4.6 %collective-permute-start.7 = (bf16[32,1536]{1,0:T(8,128)(2,1)S(1)}, bf16[32,1536]{1,0:T(8,128)(2,1)S(1)}, u32[]{:S(2)}, u32[]{:S(2)}) collective-permute-start(bf16[32,1536]{1,0:T(8,128)(2,1)S(1)} %constant_dynamic-update-slice_fusion.refs_0_), channel_id=1, source_target_pairs={{0,8},{1,9},{2,10},{3,11},{4,12},{5,13},{6,14},{7,15},{8,0},{9,1},... | collective-permute-start | bytes 294920 | tf_op jit(solution)/shard_map/ppermute | solution.py:69
  38.8 3.7 %collective-permute-start.10 = (bf16[32,1536]{1,0:T(8,128)(2,1)S(1)}, bf16[32,1536]{1,0:T(8,128)(2,1)S(1)}, u32[]{:S(2)}, u32[]{:S(2)}) collective-permute-start(bf16[32,1536]{1,0:T(8,128)(2,1)S(1)} %constant_dynamic-update-slice_fusion.refs_0_), channel_id=1, source_target_pairs={{0,4},{1,5},{2,6},{3,7},{4,0},{5,1},{6,2},{7,3},{8,12},{9,13},{10,... | collective-permute-start | bytes 294920 | tf_op jit(solution)/shard_map/ppermute | solution.py:69
  40.8 2.9 %copy-start.7 = (bf16[32,1536]{1,0:T(8,128)(2,1)}, bf16[32,1536]{1,0:T(8,128)(2,1)S(1)}, u32[]{:S(2)}) copy-start(bf16[32,1536]{1,0:T(8,128)(2,1)S(1)} %collective-permute-done.9.refs_3_) | copy-start | bytes 294916
  40.8 1.7 %collective-permute-start.13 = (bf16[32,1536]{1,0:T(8,128)(2,1)S(1)}, bf16[32,1536]{1,0:T(8,128)(2,1)S(1)}, u32[]{:S(2)}, u32[]{:S(2)}) collective-permute-start(bf16[32,1536]{1,0:T(8,128)(2,1)S(1)} %collective-permute-done.9.refs_3_), channel_id=1, source_target_pairs={{0,4},{1,5},{2,6},{3,7},{4,0},{5,1},{6,2},{7,3},{8,12},{9,13},{10,... | collective-permute-start | bytes 294920 | tf_op jit(solution)/shard_map/ppermute | solution.py:69
  41.8 1.9 %copy-start.9 = (bf16[32,1536]{1,0:T(8,128)(2,1)}, bf16[32,1536]{1,0:T(8,128)(2,1)S(1)}, u32[]{:S(2)}) copy-start(bf16[32,1536]{1,0:T(8,128)(2,1)S(1)} %collective-permute-done.8.refs_2_) | copy-start | bytes 294916
  41.8 1.3 %collective-permute-start.12 = (bf16[32,1536]{1,0:T(8,128)(2,1)S(1)}, bf16[32,1536]{1,0:T(8,128)(2,1)S(1)}, u32[]{:S(2)}, u32[]{:S(2)}) collective-permute-start(bf16[32,1536]{1,0:T(8,128)(2,1)S(1)} %collective-permute-done.8.refs_2_), channel_id=1, source_target_pairs={{0,4},{1,5},{2,6},{3,7},{4,0},{5,1},{6,2},{7,3},{8,12},{9,13},{10,... | collective-permute-start | bytes 294920 | tf_op jit(solution)/shard_map/ppermute | solution.py:69
  42.5 1.3 %copy-start.11 = (bf16[32,1536]{1,0:T(8,128)(2,1)}, bf16[32,1536]{1,0:T(8,128)(2,1)S(1)}, u32[]{:S(2)}) copy-start(bf16[32,1536]{1,0:T(8,128)(2,1)S(1)} %collective-permute-done.7.refs_1_) | copy-start | bytes 294916
  42.5 1.3 %collective-permute-start.11 = (bf16[32,1536]{1,0:T(8,128)(2,1)S(1)}, bf16[32,1536]{1,0:T(8,128)(2,1)S(1)}, u32[]{:S(2)}, u32[]{:S(2)}) collective-permute-start(bf16[32,1536]{1,0:T(8,128)(2,1)S(1)} %collective-permute-done.7.refs_1_), channel_id=1, source_target_pairs={{0,4},{1,5},{2,6},{3,7},{4,0},{5,1},{6,2},{7,3},{8,12},{9,13},{10,... | collective-permute-start | bytes 294920 | tf_op jit(solution)/shard_map/ppermute | solution.py:69
  42.5 1.3 %copy-start.13 = (bf16[32,1536]{1,0:T(8,128)(2,1)}, bf16[32,1536]{1,0:T(8,128)(2,1)S(1)}, u32[]{:S(2)}) copy-start(bf16[32,1536]{1,0:T(8,128)(2,1)S(1)} %collective-permute-done.10.refs_4_) | copy-start | bytes 294916
  42.5 1.3 %copy-start.15 = (bf16[32,1536]{1,0:T(8,128)(2,1)}, bf16[32,1536]{1,0:T(8,128)(2,1)S(1)}, u32[]{:S(2)}) copy-start(bf16[32,1536]{1,0:T(8,128)(2,1)S(1)} %collective-permute-done.13.refs_7_) | copy-start | bytes 294916
  43.1 0.7 copy-start.17
  53.8 2.0 %collective-permute-start.14 = (bf16[128,1536]{1,0:T(8,128)(2,1)}, bf16[128,1536]{1,0:T(8,128)(2,1)S(1)}, u32[]{:S(2)}, u32[]{:S(2)}) collective-permute-start(bf16[128,1536]{1,0:T(8,128)(2,1)} %get-tuple-element.38), channel_id=1, source_target_pairs={{0,4},{1,5},{2,6},{3,7},{4,0},{5,1},{6,2},{7,3},{8,12},{9,13},{10,... | collective-permute-start | bytes 1179656 | tf_op jit(solution)/shard_map/ppermute | solution.py:69
  55.8 0.7 copy-start.1
  58.4 5.2 %collective-permute-start.15 = (bf16[32,1536]{1,0:T(8,128)(2,1)}, bf16[32,1536]{1,0:T(8,128)(2,1)S(1)}, u32[]{:S(2)}, u32[]{:S(2)}) collective-permute-start(bf16[32,1536]{1,0:T(8,128)(2,1)} %get-tuple-element.40), channel_id=1, source_target_pairs={{0,8},{1,9},{2,10},{3,11},{4,12},{5,13},{6,14},{7,15},{8,0},{9,1},... | collective-permute-start | bytes 294920 | tf_op jit(solution)/shard_map/ppermute | solution.py:69
  59.5 5.9 %collective-permute-start.16 = (bf16[32,1536]{1,0:T(8,128)(2,1)}, bf16[32,1536]{1,0:T(8,128)(2,1)S(1)}, u32[]{:S(2)}, u32[]{:S(2)}) collective-permute-start(bf16[32,1536]{1,0:T(8,128)(2,1)} %get-tuple-element.41), channel_id=1, source_target_pairs={{0,16},{1,17},{2,18},{3,19},{4,20},{5,21},{6,22},{7,23},{8,24},{9,... | collective-permute-start | bytes 294920 | tf_op jit(solution)/shard_map/ppermute | solution.py:69
  60.8 5.7 %collective-permute-start.17 = (bf16[32,1536]{1,0:T(8,128)(2,1)}, bf16[32,1536]{1,0:T(8,128)(2,1)S(1)}, u32[]{:S(2)}, u32[]{:S(2)}) collective-permute-start(bf16[32,1536]{1,0:T(8,128)(2,1)} %get-tuple-element.42), channel_id=1, source_target_pairs={{0,24},{1,25},{2,26},{3,27},{4,28},{5,29},{6,30},{7,31},{8,16},{9,... | collective-permute-start | bytes 294920 | tf_op jit(solution)/shard_map/ppermute | solution.py:69
  63.6 2.9 %copy-start.21 = (bf16[32,1536]{1,0:T(8,128)(2,1)}, bf16[32,1536]{1,0:T(8,128)(2,1)S(1)}, u32[]{:S(2)}) copy-start(bf16[32,1536]{1,0:T(8,128)(2,1)S(1)} %collective-permute-done.15.refs_1_) | copy-start | bytes 294916
  65.4 1.1 %copy-start.22 = (bf16[32,1536]{1,0:T(8,128)(2,1)}, bf16[32,1536]{1,0:T(8,128)(2,1)S(1)}, u32[]{:S(2)}) copy-start(bf16[32,1536]{1,0:T(8,128)(2,1)S(1)} %collective-permute-done.16.refs_2_) | copy-start | bytes 294916
  68.8 5.1 %collective-permute-start.18 = (bf16[8,1536]{1,0:T(8,128)(2,1)}, bf16[8,1536]{1,0:T(8,128)(2,1)S(1)}, u32[]{:S(2)}, u32[]{:S(2)}) collective-permute-start(bf16[8,1536]{1,0:T(8,128)(2,1)} %get-tuple-element.44), channel_id=1, source_target_pairs={{0,1},{1,0},{2,3},{3,2},{4,5},{5,4},{6,7},{7,6},{8,9},{9,8},{10,11... | collective-permute-start | bytes 73736 | tf_op jit(solution)/shard_map/ppermute | solution.py:69
  68.8 5.1 %collective-permute-start.19 = (bf16[8,1536]{1,0:T(8,128)(2,1)}, bf16[8,1536]{1,0:T(8,128)(2,1)S(1)}, u32[]{:S(2)}, u32[]{:S(2)}) collective-permute-start(bf16[8,1536]{1,0:T(8,128)(2,1)} %get-tuple-element.45), channel_id=1, source_target_pairs={{0,2},{1,3},{2,0},{3,1},{4,6},{5,7},{6,4},{7,5},{8,10},{9,11},{10,... | collective-permute-start | bytes 73736 | tf_op jit(solution)/shard_map/ppermute | solution.py:69
  69.7 5.8 %collective-permute-start.20 = (bf16[8,1536]{1,0:T(8,128)(2,1)}, bf16[8,1536]{1,0:T(8,128)(2,1)S(1)}, u32[]{:S(2)}, u32[]{:S(2)}) collective-permute-start(bf16[8,1536]{1,0:T(8,128)(2,1)} %get-tuple-element.46), channel_id=1, source_target_pairs={{0,3},{1,2},{2,1},{3,0},{4,7},{5,6},{6,5},{7,4},{8,11},{9,10},{10,... | collective-permute-start | bytes 73736 | tf_op jit(solution)/shard_map/ppermute | solution.py:69
  75.5 8.5 %copy-start.3 = (bf16[32,1536]{1,0:T(8,128)(2,1)}, bf16[32,1536]{1,0:T(8,128)(2,1)S(1)}, u32[]{:S(2)}) copy-start(bf16[32,1536]{1,0:T(8,128)(2,1)S(1)} %constant_dynamic-update-slice_fusion.4.refs_0_) | copy-start | bytes 294916
  75.5 5.5 %collective-permute-start.23 = (bf16[32,1536]{1,0:T(8,128)(2,1)S(1)}, bf16[32,1536]{1,0:T(8,128)(2,1)S(1)}, u32[]{:S(2)}, u32[]{:S(2)}) collective-permute-start(bf16[32,1536]{1,0:T(8,128)(2,1)S(1)} %constant_dynamic-update-slice_fusion.4.refs_0_), channel_id=1, source_target_pairs={{0,24},{1,25},{2,26},{3,27},{4,28},{5,29},{6,30},{7,31},{8,16},{9,... | collective-permute-start | bytes 294920 | tf_op jit(solution)/shard_map/ppermute | solution.py:69
  77.3 4.8 %collective-permute-start.22 = (bf16[32,1536]{1,0:T(8,128)(2,1)S(1)}, bf16[32,1536]{1,0:T(8,128)(2,1)S(1)}, u32[]{:S(2)}, u32[]{:S(2)}) collective-permute-start(bf16[32,1536]{1,0:T(8,128)(2,1)S(1)} %constant_dynamic-update-slice_fusion.4.refs_0_), channel_id=1, source_target_pairs={{0,16},{1,17},{2,18},{3,19},{4,20},{5,21},{6,22},{7,23},{8,24},{9,... | collective-permute-start | bytes 294920 | tf_op jit(solution)/shard_map/ppermute | solution.py:69
  78.0 4.6 %collective-permute-start.21 = (bf16[32,1536]{1,0:T(8,128)(2,1)S(1)}, bf16[32,1536]{1,0:T(8,128)(2,1)S(1)}, u32[]{:S(2)}, u32[]{:S(2)}) collective-permute-start(bf16[32,1536]{1,0:T(8,128)(2,1)S(1)} %constant_dynamic-update-slice_fusion.4.refs_0_), channel_id=1, source_target_pairs={{0,8},{1,9},{2,10},{3,11},{4,12},{5,13},{6,14},{7,15},{8,0},{9,1},... | collective-permute-start | bytes 294920 | tf_op jit(solution)/shard_map/ppermute | solution.py:69
  79.0 3.7 %collective-permute-start.24 = (bf16[32,1536]{1,0:T(8,128)(2,1)S(1)}, bf16[32,1536]{1,0:T(8,128)(2,1)S(1)}, u32[]{:S(2)}, u32[]{:S(2)}) collective-permute-start(bf16[32,1536]{1,0:T(8,128)(2,1)S(1)} %constant_dynamic-update-slice_fusion.4.refs_0_), channel_id=1, source_target_pairs={{0,4},{1,5},{2,6},{3,7},{4,0},{5,1},{6,2},{7,3},{8,12},{9,13},{10,... | collective-permute-start | bytes 294920 | tf_op jit(solution)/shard_map/ppermute | solution.py:69
  81.0 2.9 %copy-start.8 = (bf16[32,1536]{1,0:T(8,128)(2,1)}, bf16[32,1536]{1,0:T(8,128)(2,1)S(1)}, u32[]{:S(2)}) copy-start(bf16[32,1536]{1,0:T(8,128)(2,1)S(1)} %collective-permute-done.23.refs_3_) | copy-start | bytes 294916
  81.0 1.6 %collective-permute-start.27 = (bf16[32,1536]{1,0:T(8,128)(2,1)S(1)}, bf16[32,1536]{1,0:T(8,128)(2,1)S(1)}, u32[]{:S(2)}, u32[]{:S(2)}) collective-permute-start(bf16[32,1536]{1,0:T(8,128)(2,1)S(1)} %collective-permute-done.23.refs_3_), channel_id=1, source_target_pairs={{0,4},{1,5},{2,6},{3,7},{4,0},{5,1},{6,2},{7,3},{8,12},{9,13},{10,... | collective-permute-start | bytes 294920 | tf_op jit(solution)/shard_map/ppermute | solution.py:69
  82.1 1.9 %copy-start.10 = (bf16[32,1536]{1,0:T(8,128)(2,1)}, bf16[32,1536]{1,0:T(8,128)(2,1)S(1)}, u32[]{:S(2)}) copy-start(bf16[32,1536]{1,0:T(8,128)(2,1)S(1)} %collective-permute-done.22.refs_2_) | copy-start | bytes 294916
  82.1 1.3 %collective-permute-start.26 = (bf16[32,1536]{1,0:T(8,128)(2,1)S(1)}, bf16[32,1536]{1,0:T(8,128)(2,1)S(1)}, u32[]{:S(2)}, u32[]{:S(2)}) collective-permute-start(bf16[32,1536]{1,0:T(8,128)(2,1)S(1)} %collective-permute-done.22.refs_2_), channel_id=1, source_target_pairs={{0,4},{1,5},{2,6},{3,7},{4,0},{5,1},{6,2},{7,3},{8,12},{9,13},{10,... | collective-permute-start | bytes 294920 | tf_op jit(solution)/shard_map/ppermute | solution.py:69
  82.7 1.3 %copy-start.12 = (bf16[32,1536]{1,0:T(8,128)(2,1)}, bf16[32,1536]{1,0:T(8,128)(2,1)S(1)}, u32[]{:S(2)}) copy-start(bf16[32,1536]{1,0:T(8,128)(2,1)S(1)} %collective-permute-done.21.refs_1_) | copy-start | bytes 294916
  82.7 1.3 %collective-permute-start.25 = (bf16[32,1536]{1,0:T(8,128)(2,1)S(1)}, bf16[32,1536]{1,0:T(8,128)(2,1)S(1)}, u32[]{:S(2)}, u32[]{:S(2)}) collective-permute-start(bf16[32,1536]{1,0:T(8,128)(2,1)S(1)} %collective-permute-done.21.refs_1_), channel_id=1, source_target_pairs={{0,4},{1,5},{2,6},{3,7},{4,0},{5,1},{6,2},{7,3},{8,12},{9,13},{10,... | collective-permute-start | bytes 294920 | tf_op jit(solution)/shard_map/ppermute | solution.py:69
  82.7 1.3 %copy-start.14 = (bf16[32,1536]{1,0:T(8,128)(2,1)}, bf16[32,1536]{1,0:T(8,128)(2,1)S(1)}, u32[]{:S(2)}) copy-start(bf16[32,1536]{1,0:T(8,128)(2,1)S(1)} %collective-permute-done.24.refs_4_) | copy-start | bytes 294916
  82.7 1.3 %copy-start.16 = (bf16[32,1536]{1,0:T(8,128)(2,1)}, bf16[32,1536]{1,0:T(8,128)(2,1)S(1)}, u32[]{:S(2)}) copy-start(bf16[32,1536]{1,0:T(8,128)(2,1)S(1)} %collective-permute-done.27.refs_7_) | copy-start | bytes 294916
  83.4 0.6 copy-start.18
  (4 other events, 2.5 us)

commit v2 on v1

--- a/solution.py
+++ b/solution.py
@@ -93,6 +93,12 @@
 
         def shape(*dims):
             return jax.ShapeDtypeStruct(dims, BF16)
+
+        def near(*dims):
+            return pltpu.VMEM(dims, BF16)
+
+        def keep(xs):
+            return [pltpu.with_memory_space_constraint(x, pltpu.VMEM) for x in xs]
 
         def slot_ids(dims, dim):
             k, _, z = place()
@@ -164,7 +170,7 @@
             name="dispatch",
             in_specs=[any_spec, smem_spec, vmem_spec],
             out_specs=[vmem_spec] * (minor + 1),
-            out_shape=[shape(slots, wide)] * minor + [shape(rows_here, slots)],
+            out_shape=[near(slots, wide)] * minor + [near(rows_here, slots)],
             scratch_shapes=[
                 pltpu.VMEM((minor, rows_here, width), BF16),
                 pltpu.VMEM((minor, width, slots), BF16),
@@ -188,8 +194,8 @@
             name="merge_minor",
             in_specs=[vmem_spec] * minor,
             out_specs=[vmem_spec] * major,
-            out_shape=[shape(piece, wide)] * major,
-        )(*parts)
+            out_shape=[near(piece, wide)] * major,
+        )(*keep(parts))
 
         parts = [parts[0]] + [exchange(parts[p], p, "major") for p in range(1, major)]
 
@@ -205,8 +211,8 @@
             name="merge_major",
             in_specs=[vmem_spec] * major,
             out_specs=[vmem_spec] * n_grp,
-            out_shape=[shape(grain, width)] * n_grp,
-        )(*parts)
+            out_shape=[near(grain, width)] * n_grp,
+        )(*keep(parts))
 
         def spread(parts):
             parts = [parts[0]] + [exchange(parts[q], q, "grp") for q in range(1, n_grp)]
@@ -260,14 +266,14 @@
             name="experts",
             in_specs=[vmem_spec] * (minor * major) + [any_spec] * 3,
             out_specs=[vmem_spec] * minor,
-            out_shape=[shape(major * piece, width)] * minor,
+            out_shape=[near(major * piece, width)] * minor,
             scratch_shapes=[
                 pltpu.VMEM((exp_dev, minor, width, ff), BF16),
                 pltpu.VMEM((exp_dev, minor, width, ff), BF16),
                 pltpu.VMEM((exp_dev, minor, ff, width), BF16),
                 pltpu.SemaphoreType.DMA((3, exp_dev, minor)),
             ],
-        )(*[x for group in gathered for x in group], gate_weight, up_weight, down_weight)
+        )(*keep([x for group in gathered for x in group]), gate_weight, up_weight, down_weight)
 
         parts = [parts[0]] + [exchange(parts[h], h, "minor") for h in range(1, minor)]
 
@@ -282,8 +288,8 @@
             name="add_minor",
             in_specs=[vmem_spec] * minor,
             out_specs=[vmem_spec] * major,
-            out_shape=[shape(piece, width)] * major,
-        )(*parts)
+            out_shape=[near(piece, width)] * major,
+        )(*keep(parts))
 
         parts = [parts[0]] + [exchange(parts[p], p, "major") for p in range(1, major)]
 
@@ -298,8 +304,8 @@
             name="add_major",
             in_specs=[vmem_spec] * major,
             out_specs=[vmem_spec] * n_grp,
-            out_shape=[shape(grain, width)] * n_grp,
-        )(*parts)
+            out_shape=[near(grain, width)] * n_grp,
+        )(*keep(parts))
 
         gathered = spread(parts)
 
@@ -335,7 +341,7 @@
                 pltpu.VMEM((minor, rows_here, width), BF16),
                 pltpu.SemaphoreType.DMA((chunks, minor)),
             ],
-        )(mix, *[x for group in gathered for x in group])
+        )(*keep([mix] + [x for group in gathered for x in group]))
 
     return body
 

time: 89.4 us -> 72.9 us (0.82)
  Pallas kernels: 28.7 us -> 17.8 us
  local copies, waits for them, and re-layouts: 5.54 us -> 0.02 us
    unnamed x54 -> x6, local copies, waits for them, and re-layouts: 5.53 us -> 0.02 us
    pallas_call x1, Pallas kernels: 9.28 us -> 7.3 us  [body(): pl.pallas_call(experts, name='experts', in_specs=[vmem_spec] * (minor * m...]
    pallas_call x1, Pallas kernels: 2.13 us -> 0.31 us  [body(): pl.pallas_call(merge_minor, name='merge_minor', in_specs=[vmem_spec] * mi...]
    pallas_call x1, Pallas kernels: 1.91 us -> 0.09 us  [body(): pl.pallas_call(add_minor, name='add_minor', in_specs=[vmem_spec] * minor,...]
    pallas_call x1, Pallas kernels: 1.84 us -> 0.19 us  [body(): pl.pallas_call(merge_major, name='merge_major', in_specs=[vmem_spec] * ma...]
    pallas_call x1, Pallas kernels: 1.69 us -> 0.05 us  [body(): pl.pallas_call(add_major, name='add_major', in_specs=[vmem_spec] * major,...]
    pallas_call x1, Pallas kernels: 4.34 us -> 3.08 us  [body(): pl.pallas_call(combine, name='combine', in_specs=[vmem_spec] * (1 + minor...]
  transfers between devices with their start and end apart: 28 -> 28, of which waited for: 21 -> 22; matrix products, arithmetic and copies ran while one was open for 2% -> 0% of each run, Pallas kernels for 0% -> 0%
where the time goes in v2:
time: 72.9 us; the launch traced here: 72.7 us
  waiting for transfers between devices  30 us (41%)
  starting transfers between devices  24.8 us (34%)
  Pallas kernels  17.8 us (24%)
    ppermute x28, waiting for transfers between devices, exchange(): return lax.ppermute(x, ('seq', 'grp'), pairs)  30 us
    ppermute x28, starting transfers between devices, exchange(): return lax.ppermute(x, ('seq', 'grp'), pairs)  24.8 us
    pallas_call x1, Pallas kernels, body(): pl.pallas_call(experts, name='experts', in_specs=[vmem_spec] * (minor * m...  7.3 us
    pallas_call x1, Pallas kernels, body(): pl.pallas_call(dispatch, name='dispatch', in_specs=[any_spec, smem_spec,...  6.77 us
    pallas_call x1, Pallas kernels, body(): pl.pallas_call(combine, name='combine', in_specs=[vmem_spec] * (1 + minor...  3.08 us
  transfers between devices with their start and end apart: 28, of which 22 were waited for; matrix products, arithmetic and copies ran while one was open for 0% of the time, Pallas kernels for 0%

profile of v2, /device:TPU:0, one launch (start us, length us, event | category | flops | bytes accessed | tf_op | source)
XLA Modules:
  0.0 72.7 jit_solution(4289067916061142435)
XLA Ops:
  0.0 6.8 %dispatch.1 = (bf16[128,1664]{1,0:T(8,128)(2,1)S(1)}, bf16[128,1664]{1,0:T(8,128)(2,1)S(1)}, bf16[1024,128]{1,0:T(8,128)(2,1)S(1)}) custom-call(bf16[1,1024,3072]{2,1,0:T(8,128)(2,1)} %tok_hbm.1, s32[1,8]{1,0:T(1,128)} %map_ref.1, bf16[3072,128]{1,0:T(8,128)(2,1)} %keys_ref.1), custom_call_target="tpu_custom_call" | custom-call | tf_op jit(solution)/shard_map/dispatch/pallas_call | solution.py:168
  6.8 0.6 collective-permute-start
  7.3 1.4 %collective-permute-done.refs_1_ = bf16[128,1664]{1,0:T(8,128)(2,1)S(1)} collective-permute-done((bf16[128,1664]{1,0:T(8,128)(2,1)S(1)}, bf16[128,1664]{1,0:T(8,128)(2,1)S(1)}, u32[]{:S(2)}, u32[]{:S(2)}) %collective-permute-start) | collective-permute-done | bytes 426016 | tf_op jit(solution)/shard_map/ppermute | solution.py:69
  8.7 0.3 merge_minor.1
  9.0 2.9 %collective-permute-start.1 = (bf16[32,1664]{1,0:T(8,128)(2,1)S(1)}, bf16[32,1664]{1,0:T(8,128)(2,1)S(1)}, u32[]{:S(2)}, u32[]{:S(2)}) collective-permute-start(bf16[32,1664]{1,0:T(8,128)(2,1)S(1)} %get-tuple-element.30), channel_id=1, source_target_pairs={{0,8},{1,9},{2,10},{3,11},{4,12},{5,13},{6,14},{7,15},{8,0},{9,1},... | collective-permute-start | bytes 319496 | tf_op jit(solution)/shard_map/ppermute | solution.py:69
  12.0 1.5 %collective-permute-start.2 = (bf16[32,1664]{1,0:T(8,128)(2,1)S(1)}, bf16[32,1664]{1,0:T(8,128)(2,1)S(1)}, u32[]{:S(2)}, u32[]{:S(2)}) collective-permute-start(bf16[32,1664]{1,0:T(8,128)(2,1)S(1)} %get-tuple-element.31), channel_id=1, source_target_pairs={{0,16},{1,17},{2,18},{3,19},{4,20},{5,21},{6,22},{7,23},{8,24},{9,... | collective-permute-start | bytes 319496 | tf_op jit(solution)/shard_map/ppermute | solution.py:69
  13.5 1.8 %collective-permute-done.1.refs_1_ = bf16[32,1664]{1,0:T(8,128)(2,1)S(1)} collective-permute-done((bf16[32,1664]{1,0:T(8,128)(2,1)S(1)}, bf16[32,1664]{1,0:T(8,128)(2,1)S(1)}, u32[]{:S(2)}, u32[]{:S(2)}) %collective-permute-start.1) | collective-permute-done | bytes 106528 | tf_op jit(solution)/shard_map/ppermute | solution.py:69
  15.3 2.7 %collective-permute-done.2.refs_2_ = bf16[32,1664]{1,0:T(8,128)(2,1)S(1)} collective-permute-done((bf16[32,1664]{1,0:T(8,128)(2,1)S(1)}, bf16[32,1664]{1,0:T(8,128)(2,1)S(1)}, u32[]{:S(2)}, u32[]{:S(2)}) %collective-permute-start.2) | collective-permute-done | bytes 106528 | tf_op jit(solution)/shard_map/ppermute | solution.py:69
  18.0 1.1 %collective-permute-done.3.refs_3_ = bf16[32,1664]{1,0:T(8,128)(2,1)S(1)} collective-permute-done((bf16[32,1664]{1,0:T(8,128)(2,1)S(1)}, bf16[32,1664]{1,0:T(8,128)(2,1)S(1)}, u32[]{:S(2)}, u32[]{:S(2)}) %collective-permute-start.3) | collective-permute-done | bytes 106528 | tf_op jit(solution)/shard_map/ppermute | solution.py:69
  19.1 0.2 merge_major.1
  19.3 1.6 %collective-permute-start.4 = (bf16[8,1536]{1,0:T(8,128)(2,1)S(1)}, bf16[8,1536]{1,0:T(8,128)(2,1)S(1)}, u32[]{:S(2)}, u32[]{:S(2)}) collective-permute-start(bf16[8,1536]{1,0:T(8,128)(2,1)S(1)} %get-tuple-element.34), channel_id=1, source_target_pairs={{0,1},{1,0},{2,3},{3,2},{4,5},{5,4},{6,7},{7,6},{8,9},{9,8},{10,11... | collective-permute-start | bytes 73736 | tf_op jit(solution)/shard_map/ppermute | solution.py:69
  20.9 2.6 %collective-permute-start.5 = (bf16[8,1536]{1,0:T(8,128)(2,1)S(1)}, bf16[8,1536]{1,0:T(8,128)(2,1)S(1)}, u32[]{:S(2)}, u32[]{:S(2)}) collective-permute-start(bf16[8,1536]{1,0:T(8,128)(2,1)S(1)} %get-tuple-element.35), channel_id=1, source_target_pairs={{0,2},{1,3},{2,0},{3,1},{4,6},{5,7},{6,4},{7,5},{8,10},{9,11},{10,... | collective-permute-start | bytes 73736 | tf_op jit(solution)/shard_map/ppermute | solution.py:69
  23.5 0.2 collective-permute-start.6
  23.7 2.1 %collective-permute-done.5 = bf16[8,1536]{1,0:T(8,128)(2,1)S(1)} collective-permute-done((bf16[8,1536]{1,0:T(8,128)(2,1)S(1)}, bf16[8,1536]{1,0:T(8,128)(2,1)S(1)}, u32[]{:S(2)}, u32[]{:S(2)}) %collective-permute-start.5) | collective-permute-done | bytes 24608 | tf_op jit(solution)/shard_map/ppermute | solution.py:69
  25.8 3.3 %collective-permute-done.6 = bf16[8,1536]{1,0:T(8,128)(2,1)S(1)} collective-permute-done((bf16[8,1536]{1,0:T(8,128)(2,1)S(1)}, bf16[8,1536]{1,0:T(8,128)(2,1)S(1)}, u32[]{:S(2)}, u32[]{:S(2)}) %collective-permute-start.6) | collective-permute-done | bytes 24608 | tf_op jit(solution)/shard_map/ppermute | solution.py:69
  29.1 1.4 %collective-permute-start.9 = (bf16[32,1536]{1,0:T(8,128)(2,1)S(1)}, bf16[32,1536]{1,0:T(8,128)(2,1)S(1)}, u32[]{:S(2)}, u32[]{:S(2)}) collective-permute-start(bf16[32,1536]{1,0:T(8,128)(2,1)S(1)} %constant_dynamic-update-slice_fusion.refs_0_), channel_id=1, source_target_pairs={{0,24},{1,25},{2,26},{3,27},{4,28},{5,29},{6,30},{7,31},{8,16},{9,... | collective-permute-start | bytes 294920 | tf_op jit(solution)/shard_map/ppermute | solution.py:69
  30.5 1.2 %collective-permute-start.8 = (bf16[32,1536]{1,0:T(8,128)(2,1)S(1)}, bf16[32,1536]{1,0:T(8,128)(2,1)S(1)}, u32[]{:S(2)}, u32[]{:S(2)}) collective-permute-start(bf16[32,1536]{1,0:T(8,128)(2,1)S(1)} %constant_dynamic-update-slice_fusion.refs_0_), channel_id=1, source_target_pairs={{0,16},{1,17},{2,18},{3,19},{4,20},{5,21},{6,22},{7,23},{8,24},{9,... | collective-permute-start | bytes 294920 | tf_op jit(solution)/shard_map/ppermute | solution.py:69
  31.7 0.9 %collective-permute-start.7 = (bf16[32,1536]{1,0:T(8,128)(2,1)S(1)}, bf16[32,1536]{1,0:T(8,128)(2,1)S(1)}, u32[]{:S(2)}, u32[]{:S(2)}) collective-permute-start(bf16[32,1536]{1,0:T(8,128)(2,1)S(1)} %constant_dynamic-update-slice_fusion.refs_0_), channel_id=1, source_target_pairs={{0,8},{1,9},{2,10},{3,11},{4,12},{5,13},{6,14},{7,15},{8,0},{9,1},... | collective-permute-start | bytes 294920 | tf_op jit(solution)/shard_map/ppermute | solution.py:69
  32.6 2.1 %collective-permute-done.9.refs_3_ = bf16[32,1536]{1,0:T(8,128)(2,1)S(1)} collective-permute-done((bf16[32,1536]{1,0:T(8,128)(2,1)S(1)}, bf16[32,1536]{1,0:T(8,128)(2,1)S(1)}, u32[]{:S(2)}, u32[]{:S(2)}) %collective-permute-start.9) | collective-permute-done | bytes 98336 | tf_op jit(solution)/shard_map/ppermute | solution.py:69
  34.7 1.0 %collective-permute-done.8.refs_2_ = bf16[32,1536]{1,0:T(8,128)(2,1)S(1)} collective-permute-done((bf16[32,1536]{1,0:T(8,128)(2,1)S(1)}, bf16[32,1536]{1,0:T(8,128)(2,1)S(1)}, u32[]{:S(2)}, u32[]{:S(2)}) %collective-permute-start.8) | collective-permute-done | bytes 98336 | tf_op jit(solution)/shard_map/ppermute | solution.py:69
  35.7 0.6 collective-permute-done.7.refs_1_
  36.4 0.7 collective-permute-done.12.refs_6_
  37.0 0.6 collective-permute-done.11.refs_5_
  37.7 7.3 %experts.1 = (bf16[128,1536]{1,0:T(8,128)(2,1)S(1)}, bf16[128,1536]{1,0:T(8,128)(2,1)S(1)}) custom-call(bf16[32,1536]{1,0:T(8,128)(2,1)S(1)} %constant_dynamic-update-slice_fusion.refs_0_, bf16[32,1536]{1,0:T(8,128)(2,1)S(1)} %collective-permute-done.7.refs_1_, bf16[32,1536]{1,0:T(8,128)(2,1)S(1)} %collective-permute-done.8.refs_2_, ...), custom_call_target="tpu_custom_call" | custom-call | tf_op jit(solution)/shard_map/experts/pallas_call | solution.py:264
  45.0 0.2 collective-permute-start.14
  45.2 1.6 %collective-permute-done.14.refs_1_ = bf16[128,1536]{1,0:T(8,128)(2,1)S(1)} collective-permute-done((bf16[128,1536]{1,0:T(8,128)(2,1)S(1)}, bf16[128,1536]{1,0:T(8,128)(2,1)S(1)}, u32[]{:S(2)}, u32[]{:S(2)}) %collective-permute-start.14) | collective-permute-done | bytes 393248 | tf_op jit(solution)/shard_map/ppermute | solution.py:69
  46.7 0.1 add_minor.1
  46.8 1.0 %collective-permute-start.15 = (bf16[32,1536]{1,0:T(8,128)(2,1)S(1)}, bf16[32,1536]{1,0:T(8,128)(2,1)S(1)}, u32[]{:S(2)}, u32[]{:S(2)}) collective-permute-start(bf16[32,1536]{1,0:T(8,128)(2,1)S(1)} %get-tuple-element.40), channel_id=1, source_target_pairs={{0,8},{1,9},{2,10},{3,11},{4,12},{5,13},{6,14},{7,15},{8,0},{9,1},... | collective-permute-start | bytes 294920 | tf_op jit(solution)/shard_map/ppermute | solution.py:69
  47.8 1.4 %collective-permute-start.16 = (bf16[32,1536]{1,0:T(8,128)(2,1)S(1)}, bf16[32,1536]{1,0:T(8,128)(2,1)S(1)}, u32[]{:S(2)}, u32[]{:S(2)}) collective-permute-start(bf16[32,1536]{1,0:T(8,128)(2,1)S(1)} %get-tuple-element.41), channel_id=1, source_target_pairs={{0,16},{1,17},{2,18},{3,19},{4,20},{5,21},{6,22},{7,23},{8,24},{9,... | collective-permute-start | bytes 294920 | tf_op jit(solution)/shard_map/ppermute | solution.py:69
  49.2 1.2 %collective-permute-start.17 = (bf16[32,1536]{1,0:T(8,128)(2,1)S(1)}, bf16[32,1536]{1,0:T(8,128)(2,1)S(1)}, u32[]{:S(2)}, u32[]{:S(2)}) collective-permute-start(bf16[32,1536]{1,0:T(8,128)(2,1)S(1)} %get-tuple-element.42), channel_id=1, source_target_pairs={{0,24},{1,25},{2,26},{3,27},{4,28},{5,29},{6,30},{7,31},{8,16},{9,... | collective-permute-start | bytes 294920 | tf_op jit(solution)/shard_map/ppermute | solution.py:69
  50.4 1.7 %collective-permute-done.15.refs_1_ = bf16[32,1536]{1,0:T(8,128)(2,1)S(1)} collective-permute-done((bf16[32,1536]{1,0:T(8,128)(2,1)S(1)}, bf16[32,1536]{1,0:T(8,128)(2,1)S(1)}, u32[]{:S(2)}, u32[]{:S(2)}) %collective-permute-start.15) | collective-permute-done | bytes 98336 | tf_op jit(solution)/shard_map/ppermute | solution.py:69
  52.1 1.4 %collective-permute-done.16.refs_2_ = bf16[32,1536]{1,0:T(8,128)(2,1)S(1)} collective-permute-done((bf16[32,1536]{1,0:T(8,128)(2,1)S(1)}, bf16[32,1536]{1,0:T(8,128)(2,1)S(1)}, u32[]{:S(2)}, u32[]{:S(2)}) %collective-permute-start.16) | collective-permute-done | bytes 98336 | tf_op jit(solution)/shard_map/ppermute | solution.py:69
  53.5 1.2 %collective-permute-done.17.refs_3_ = bf16[32,1536]{1,0:T(8,128)(2,1)S(1)} collective-permute-done((bf16[32,1536]{1,0:T(8,128)(2,1)S(1)}, bf16[32,1536]{1,0:T(8,128)(2,1)S(1)}, u32[]{:S(2)}, u32[]{:S(2)}) %collective-permute-start.17) | collective-permute-done | bytes 98336 | tf_op jit(solution)/shard_map/ppermute | solution.py:69
  54.8 0.1 collective-permute-start.18
  54.9 0.8 %collective-permute-start.19 = (bf16[8,1536]{1,0:T(8,128)(2,1)S(1)}, bf16[8,1536]{1,0:T(8,128)(2,1)S(1)}, u32[]{:S(2)}, u32[]{:S(2)}) collective-permute-start(bf16[8,1536]{1,0:T(8,128)(2,1)S(1)} %get-tuple-element.45), channel_id=1, source_target_pairs={{0,2},{1,3},{2,0},{3,1},{4,6},{5,7},{6,4},{7,5},{8,10},{9,11},{10,... | collective-permute-start | bytes 73736 | tf_op jit(solution)/shard_map/ppermute | solution.py:69
  55.7 3.6 %collective-permute-start.20 = (bf16[8,1536]{1,0:T(8,128)(2,1)S(1)}, bf16[8,1536]{1,0:T(8,128)(2,1)S(1)}, u32[]{:S(2)}, u32[]{:S(2)}) collective-permute-start(bf16[8,1536]{1,0:T(8,128)(2,1)S(1)} %get-tuple-element.46), channel_id=1, source_target_pairs={{0,3},{1,2},{2,1},{3,0},{4,7},{5,6},{6,5},{7,4},{8,11},{9,10},{10,... | collective-permute-start | bytes 73736 | tf_op jit(solution)/shard_map/ppermute | solution.py:69
  59.3 0.4 collective-permute-done.19
  59.7 1.6 %collective-permute-done.20 = bf16[8,1536]{1,0:T(8,128)(2,1)S(1)} collective-permute-done((bf16[8,1536]{1,0:T(8,128)(2,1)S(1)}, bf16[8,1536]{1,0:T(8,128)(2,1)S(1)}, u32[]{:S(2)}, u32[]{:S(2)}) %collective-permute-start.20) | collective-permute-done | bytes 24608 | tf_op jit(solution)/shard_map/ppermute | solution.py:69
  61.3 1.5 %collective-permute-start.23 = (bf16[32,1536]{1,0:T(8,128)(2,1)S(1)}, bf16[32,1536]{1,0:T(8,128)(2,1)S(1)}, u32[]{:S(2)}, u32[]{:S(2)}) collective-permute-start(bf16[32,1536]{1,0:T(8,128)(2,1)S(1)} %constant_dynamic-update-slice_fusion.4.refs_0_), channel_id=1, source_target_pairs={{0,24},{1,25},{2,26},{3,27},{4,28},{5,29},{6,30},{7,31},{8,16},{9,... | collective-permute-start | bytes 294920 | tf_op jit(solution)/shard_map/ppermute | solution.py:69
  62.8 0.9 %collective-permute-start.22 = (bf16[32,1536]{1,0:T(8,128)(2,1)S(1)}, bf16[32,1536]{1,0:T(8,128)(2,1)S(1)}, u32[]{:S(2)}, u32[]{:S(2)}) collective-permute-start(bf16[32,1536]{1,0:T(8,128)(2,1)S(1)} %constant_dynamic-update-slice_fusion.4.refs_0_), channel_id=1, source_target_pairs={{0,16},{1,17},{2,18},{3,19},{4,20},{5,21},{6,22},{7,23},{8,24},{9,... | collective-permute-start | bytes 294920 | tf_op jit(solution)/shard_map/ppermute | solution.py:69
  63.7 1.1 %collective-permute-start.21 = (bf16[32,1536]{1,0:T(8,128)(2,1)S(1)}, bf16[32,1536]{1,0:T(8,128)(2,1)S(1)}, u32[]{:S(2)}, u32[]{:S(2)}) collective-permute-start(bf16[32,1536]{1,0:T(8,128)(2,1)S(1)} %constant_dynamic-update-slice_fusion.4.refs_0_), channel_id=1, source_target_pairs={{0,8},{1,9},{2,10},{3,11},{4,12},{5,13},{6,14},{7,15},{8,0},{9,1},... | collective-permute-start | bytes 294920 | tf_op jit(solution)/shard_map/ppermute | solution.py:69
  64.8 2.1 %collective-permute-done.23.refs_3_ = bf16[32,1536]{1,0:T(8,128)(2,1)S(1)} collective-permute-done((bf16[32,1536]{1,0:T(8,128)(2,1)S(1)}, bf16[32,1536]{1,0:T(8,128)(2,1)S(1)}, u32[]{:S(2)}, u32[]{:S(2)}) %collective-permute-start.23) | collective-permute-done | bytes 98336 | tf_op jit(solution)/shard_map/ppermute | solution.py:69
  66.9 1.0 %collective-permute-done.22.refs_2_ = bf16[32,1536]{1,0:T(8,128)(2,1)S(1)} collective-permute-done((bf16[32,1536]{1,0:T(8,128)(2,1)S(1)}, bf16[32,1536]{1,0:T(8,128)(2,1)S(1)}, u32[]{:S(2)}, u32[]{:S(2)}) %collective-permute-start.22) | collective-permute-done | bytes 98336 | tf_op jit(solution)/shard_map/ppermute | solution.py:69
  67.9 0.4 collective-permute-done.21.refs_1_
  68.3 0.1 collective-permute-start.25
  68.4 0.8 %collective-permute-done.26.refs_6_ = bf16[32,1536]{1,0:T(8,128)(2,1)S(1)} collective-permute-done((bf16[32,1536]{1,0:T(8,128)(2,1)S(1)}, bf16[32,1536]{1,0:T(8,128)(2,1)S(1)}, u32[]{:S(2)}, u32[]{:S(2)}) %collective-permute-start.26) | collective-permute-done | bytes 98336 | tf_op jit(solution)/shard_map/ppermute | solution.py:69
  69.2 0.4 collective-permute-done.25.refs_5_
  69.6 3.1 %combine.1 = bf16[1,1024,3072]{2,1,0:T(8,128)(2,1)} custom-call(bf16[1024,128]{1,0:T(8,128)(2,1)S(1)} %get-tuple-element.26.mix_ref, bf16[32,1536]{1,0:T(8,128)(2,1)S(1)} %constant_dynamic-update-slice_fusion.4.refs_0_, bf16[32,1536]{1,0:T(8,128)(2,1)S(1)} %collective-permute-done.21.refs_1_, bf16[32,1536]{1,0:T(8,128)(2,1)S(1)} %collective-permute-done.22.refs_2_, ...), custom_call_target="tpu_custom_call" | custom-call | tf_op jit(solution)/shard_map/combine/pallas_call | solution.py:334
  (23 shorter events, 0.1 us)
Async XLA Ops:
  6.8 2.0 %collective-permute-start = (bf16[128,1664]{1,0:T(8,128)(2,1)S(1)}, bf16[128,1664]{1,0:T(8,128)(2,1)S(1)}, u32[]{:S(2)}, u32[]{:S(2)}) collective-permute-start(bf16[128,1664]{1,0:T(8,128)(2,1)S(1)} %get-tuple-element.28), channel_id=1, source_target_pairs={{0,4},{1,5},{2,6},{3,7},{4,0},{5,1},{6,2},{7,3},{8,12},{9,13},{10,... | collective-permute-start | bytes 1277960 | tf_op jit(solution)/shard_map/ppermute | solution.py:69
  9.0 6.3 %collective-permute-start.1 = (bf16[32,1664]{1,0:T(8,128)(2,1)S(1)}, bf16[32,1664]{1,0:T(8,128)(2,1)S(1)}, u32[]{:S(2)}, u32[]{:S(2)}) collective-permute-start(bf16[32,1664]{1,0:T(8,128)(2,1)S(1)} %get-tuple-element.30), channel_id=1, source_target_pairs={{0,8},{1,9},{2,10},{3,11},{4,12},{5,13},{6,14},{7,15},{8,0},{9,1},... | collective-permute-start | bytes 319496 | tf_op jit(solution)/shard_map/ppermute | solution.py:69
  12.0 6.1 %collective-permute-start.2 = (bf16[32,1664]{1,0:T(8,128)(2,1)S(1)}, bf16[32,1664]{1,0:T(8,128)(2,1)S(1)}, u32[]{:S(2)}, u32[]{:S(2)}) collective-permute-start(bf16[32,1664]{1,0:T(8,128)(2,1)S(1)} %get-tuple-element.31), channel_id=1, source_target_pairs={{0,16},{1,17},{2,18},{3,19},{4,20},{5,21},{6,22},{7,23},{8,24},{9,... | collective-permute-start | bytes 319496 | tf_op jit(solution)/shard_map/ppermute | solution.py:69
  13.5 5.6 %collective-permute-start.3 = (bf16[32,1664]{1,0:T(8,128)(2,1)S(1)}, bf16[32,1664]{1,0:T(8,128)(2,1)S(1)}, u32[]{:S(2)}, u32[]{:S(2)}) collective-permute-start(bf16[32,1664]{1,0:T(8,128)(2,1)S(1)} %get-tuple-element.32), channel_id=1, source_target_pairs={{0,24},{1,25},{2,26},{3,27},{4,28},{5,29},{6,30},{7,31},{8,16},{9,... | collective-permute-start | bytes 319496 | tf_op jit(solution)/shard_map/ppermute | solution.py:69
  19.3 4.5 %collective-permute-start.4 = (bf16[8,1536]{1,0:T(8,128)(2,1)S(1)}, bf16[8,1536]{1,0:T(8,128)(2,1)S(1)}, u32[]{:S(2)}, u32[]{:S(2)}) collective-permute-start(bf16[8,1536]{1,0:T(8,128)(2,1)S(1)} %get-tuple-element.34), channel_id=1, source_target_pairs={{0,1},{1,0},{2,3},{3,2},{4,5},{5,4},{6,7},{7,6},{8,9},{9,8},{10,11... | collective-permute-start | bytes 73736 | tf_op jit(solution)/shard_map/ppermute | solution.py:69
  20.9 4.9 %collective-permute-start.5 = (bf16[8,1536]{1,0:T(8,128)(2,1)S(1)}, bf16[8,1536]{1,0:T(8,128)(2,1)S(1)}, u32[]{:S(2)}, u32[]{:S(2)}) collective-permute-start(bf16[8,1536]{1,0:T(8,128)(2,1)S(1)} %get-tuple-element.35), channel_id=1, source_target_pairs={{0,2},{1,3},{2,0},{3,1},{4,6},{5,7},{6,4},{7,5},{8,10},{9,11},{10,... | collective-permute-start | bytes 73736 | tf_op jit(solution)/shard_map/ppermute | solution.py:69
  23.5 5.6 %collective-permute-start.6 = (bf16[8,1536]{1,0:T(8,128)(2,1)S(1)}, bf16[8,1536]{1,0:T(8,128)(2,1)S(1)}, u32[]{:S(2)}, u32[]{:S(2)}) collective-permute-start(bf16[8,1536]{1,0:T(8,128)(2,1)S(1)} %get-tuple-element.36), channel_id=1, source_target_pairs={{0,3},{1,2},{2,1},{3,0},{4,7},{5,6},{6,5},{7,4},{8,11},{9,10},{10,... | collective-permute-start | bytes 73736 | tf_op jit(solution)/shard_map/ppermute | solution.py:69
  29.1 5.6 %collective-permute-start.9 = (bf16[32,1536]{1,0:T(8,128)(2,1)S(1)}, bf16[32,1536]{1,0:T(8,128)(2,1)S(1)}, u32[]{:S(2)}, u32[]{:S(2)}) collective-permute-start(bf16[32,1536]{1,0:T(8,128)(2,1)S(1)} %constant_dynamic-update-slice_fusion.refs_0_), channel_id=1, source_target_pairs={{0,24},{1,25},{2,26},{3,27},{4,28},{5,29},{6,30},{7,31},{8,16},{9,... | collective-permute-start | bytes 294920 | tf_op jit(solution)/shard_map/ppermute | solution.py:69
  30.5 5.2 %collective-permute-start.8 = (bf16[32,1536]{1,0:T(8,128)(2,1)S(1)}, bf16[32,1536]{1,0:T(8,128)(2,1)S(1)}, u32[]{:S(2)}, u32[]{:S(2)}) collective-permute-start(bf16[32,1536]{1,0:T(8,128)(2,1)S(1)} %constant_dynamic-update-slice_fusion.refs_0_), channel_id=1, source_target_pairs={{0,16},{1,17},{2,18},{3,19},{4,20},{5,21},{6,22},{7,23},{8,24},{9,... | collective-permute-start | bytes 294920 | tf_op jit(solution)/shard_map/ppermute | solution.py:69
  31.7 4.6 %collective-permute-start.7 = (bf16[32,1536]{1,0:T(8,128)(2,1)S(1)}, bf16[32,1536]{1,0:T(8,128)(2,1)S(1)}, u32[]{:S(2)}, u32[]{:S(2)}) collective-permute-start(bf16[32,1536]{1,0:T(8,128)(2,1)S(1)} %constant_dynamic-update-slice_fusion.refs_0_), channel_id=1, source_target_pairs={{0,8},{1,9},{2,10},{3,11},{4,12},{5,13},{6,14},{7,15},{8,0},{9,1},... | collective-permute-start | bytes 294920 | tf_op jit(solution)/shard_map/ppermute | solution.py:69
  32.6 3.7 %collective-permute-start.10 = (bf16[32,1536]{1,0:T(8,128)(2,1)S(1)}, bf16[32,1536]{1,0:T(8,128)(2,1)S(1)}, u32[]{:S(2)}, u32[]{:S(2)}) collective-permute-start(bf16[32,1536]{1,0:T(8,128)(2,1)S(1)} %constant_dynamic-update-slice_fusion.refs_0_), channel_id=1, source_target_pairs={{0,4},{1,5},{2,6},{3,7},{4,0},{5,1},{6,2},{7,3},{8,12},{9,13},{10,... | collective-permute-start | bytes 294920 | tf_op jit(solution)/shard_map/ppermute | solution.py:69
  34.7 1.6 %collective-permute-start.13 = (bf16[32,1536]{1,0:T(8,128)(2,1)S(1)}, bf16[32,1536]{1,0:T(8,128)(2,1)S(1)}, u32[]{:S(2)}, u32[]{:S(2)}) collective-permute-start(bf16[32,1536]{1,0:T(8,128)(2,1)S(1)} %collective-permute-done.9.refs_3_), channel_id=1, source_target_pairs={{0,4},{1,5},{2,6},{3,7},{4,0},{5,1},{6,2},{7,3},{8,12},{9,13},{10,... | collective-permute-start | bytes 294920 | tf_op jit(solution)/shard_map/ppermute | solution.py:69
  35.7 1.3 %collective-permute-start.12 = (bf16[32,1536]{1,0:T(8,128)(2,1)S(1)}, bf16[32,1536]{1,0:T(8,128)(2,1)S(1)}, u32[]{:S(2)}, u32[]{:S(2)}) collective-permute-start(bf16[32,1536]{1,0:T(8,128)(2,1)S(1)} %collective-permute-done.8.refs_2_), channel_id=1, source_target_pairs={{0,4},{1,5},{2,6},{3,7},{4,0},{5,1},{6,2},{7,3},{8,12},{9,13},{10,... | collective-permute-start | bytes 294920 | tf_op jit(solution)/shard_map/ppermute | solution.py:69
  36.4 1.3 %collective-permute-start.11 = (bf16[32,1536]{1,0:T(8,128)(2,1)S(1)}, bf16[32,1536]{1,0:T(8,128)(2,1)S(1)}, u32[]{:S(2)}, u32[]{:S(2)}) collective-permute-start(bf16[32,1536]{1,0:T(8,128)(2,1)S(1)} %collective-permute-done.7.refs_1_), channel_id=1, source_target_pairs={{0,4},{1,5},{2,6},{3,7},{4,0},{5,1},{6,2},{7,3},{8,12},{9,13},{10,... | collective-permute-start | bytes 294920 | tf_op jit(solution)/shard_map/ppermute | solution.py:69
  45.0 1.8 %collective-permute-start.14 = (bf16[128,1536]{1,0:T(8,128)(2,1)S(1)}, bf16[128,1536]{1,0:T(8,128)(2,1)S(1)}, u32[]{:S(2)}, u32[]{:S(2)}) collective-permute-start(bf16[128,1536]{1,0:T(8,128)(2,1)S(1)} %get-tuple-element.38), channel_id=1, source_target_pairs={{0,4},{1,5},{2,6},{3,7},{4,0},{5,1},{6,2},{7,3},{8,12},{9,13},{10,... | collective-permute-start | bytes 1179656 | tf_op jit(solution)/shard_map/ppermute | solution.py:69
  46.8 5.2 %collective-permute-start.15 = (bf16[32,1536]{1,0:T(8,128)(2,1)S(1)}, bf16[32,1536]{1,0:T(8,128)(2,1)S(1)}, u32[]{:S(2)}, u32[]{:S(2)}) collective-permute-start(bf16[32,1536]{1,0:T(8,128)(2,1)S(1)} %get-tuple-element.40), channel_id=1, source_target_pairs={{0,8},{1,9},{2,10},{3,11},{4,12},{5,13},{6,14},{7,15},{8,0},{9,1},... | collective-permute-start | bytes 294920 | tf_op jit(solution)/shard_map/ppermute | solution.py:69
  47.8 5.7 %collective-permute-start.16 = (bf16[32,1536]{1,0:T(8,128)(2,1)S(1)}, bf16[32,1536]{1,0:T(8,128)(2,1)S(1)}, u32[]{:S(2)}, u32[]{:S(2)}) collective-permute-start(bf16[32,1536]{1,0:T(8,128)(2,1)S(1)} %get-tuple-element.41), channel_id=1, source_target_pairs={{0,16},{1,17},{2,18},{3,19},{4,20},{5,21},{6,22},{7,23},{8,24},{9,... | collective-permute-start | bytes 294920 | tf_op jit(solution)/shard_map/ppermute | solution.py:69
  49.2 5.5 %collective-permute-start.17 = (bf16[32,1536]{1,0:T(8,128)(2,1)S(1)}, bf16[32,1536]{1,0:T(8,128)(2,1)S(1)}, u32[]{:S(2)}, u32[]{:S(2)}) collective-permute-start(bf16[32,1536]{1,0:T(8,128)(2,1)S(1)} %get-tuple-element.42), channel_id=1, source_target_pairs={{0,24},{1,25},{2,26},{3,27},{4,28},{5,29},{6,30},{7,31},{8,16},{9,... | collective-permute-start | bytes 294920 | tf_op jit(solution)/shard_map/ppermute | solution.py:69
  54.8 4.5 %collective-permute-start.18 = (bf16[8,1536]{1,0:T(8,128)(2,1)S(1)}, bf16[8,1536]{1,0:T(8,128)(2,1)S(1)}, u32[]{:S(2)}, u32[]{:S(2)}) collective-permute-start(bf16[8,1536]{1,0:T(8,128)(2,1)S(1)} %get-tuple-element.44), channel_id=1, source_target_pairs={{0,1},{1,0},{2,3},{3,2},{4,5},{5,4},{6,7},{7,6},{8,9},{9,8},{10,11... | collective-permute-start | bytes 73736 | tf_op jit(solution)/shard_map/ppermute | solution.py:69
  54.9 4.8 %collective-permute-start.19 = (bf16[8,1536]{1,0:T(8,128)(2,1)S(1)}, bf16[8,1536]{1,0:T(8,128)(2,1)S(1)}, u32[]{:S(2)}, u32[]{:S(2)}) collective-permute-start(bf16[8,1536]{1,0:T(8,128)(2,1)S(1)} %get-tuple-element.45), channel_id=1, source_target_pairs={{0,2},{1,3},{2,0},{3,1},{4,6},{5,7},{6,4},{7,5},{8,10},{9,11},{10,... | collective-permute-start | bytes 73736 | tf_op jit(solution)/shard_map/ppermute | solution.py:69
  55.7 5.6 %collective-permute-start.20 = (bf16[8,1536]{1,0:T(8,128)(2,1)S(1)}, bf16[8,1536]{1,0:T(8,128)(2,1)S(1)}, u32[]{:S(2)}, u32[]{:S(2)}) collective-permute-start(bf16[8,1536]{1,0:T(8,128)(2,1)S(1)} %get-tuple-element.46), channel_id=1, source_target_pairs={{0,3},{1,2},{2,1},{3,0},{4,7},{5,6},{6,5},{7,4},{8,11},{9,10},{10,... | collective-permute-start | bytes 73736 | tf_op jit(solution)/shard_map/ppermute | solution.py:69
  61.3 5.6 %collective-permute-start.23 = (bf16[32,1536]{1,0:T(8,128)(2,1)S(1)}, bf16[32,1536]{1,0:T(8,128)(2,1)S(1)}, u32[]{:S(2)}, u32[]{:S(2)}) collective-permute-start(bf16[32,1536]{1,0:T(8,128)(2,1)S(1)} %constant_dynamic-update-slice_fusion.4.refs_0_), channel_id=1, source_target_pairs={{0,24},{1,25},{2,26},{3,27},{4,28},{5,29},{6,30},{7,31},{8,16},{9,... | collective-permute-start | bytes 294920 | tf_op jit(solution)/shard_map/ppermute | solution.py:69
  62.8 5.1 %collective-permute-start.22 = (bf16[32,1536]{1,0:T(8,128)(2,1)S(1)}, bf16[32,1536]{1,0:T(8,128)(2,1)S(1)}, u32[]{:S(2)}, u32[]{:S(2)}) collective-permute-start(bf16[32,1536]{1,0:T(8,128)(2,1)S(1)} %constant_dynamic-update-slice_fusion.4.refs_0_), channel_id=1, source_target_pairs={{0,16},{1,17},{2,18},{3,19},{4,20},{5,21},{6,22},{7,23},{8,24},{9,... | collective-permute-start | bytes 294920 | tf_op jit(solution)/shard_map/ppermute | solution.py:69
  63.7 4.6 %collective-permute-start.21 = (bf16[32,1536]{1,0:T(8,128)(2,1)S(1)}, bf16[32,1536]{1,0:T(8,128)(2,1)S(1)}, u32[]{:S(2)}, u32[]{:S(2)}) collective-permute-start(bf16[32,1536]{1,0:T(8,128)(2,1)S(1)} %constant_dynamic-update-slice_fusion.4.refs_0_), channel_id=1, source_target_pairs={{0,8},{1,9},{2,10},{3,11},{4,12},{5,13},{6,14},{7,15},{8,0},{9,1},... | collective-permute-start | bytes 294920 | tf_op jit(solution)/shard_map/ppermute | solution.py:69
  64.8 3.6 %collective-permute-start.24 = (bf16[32,1536]{1,0:T(8,128)(2,1)S(1)}, bf16[32,1536]{1,0:T(8,128)(2,1)S(1)}, u32[]{:S(2)}, u32[]{:S(2)}) collective-permute-start(bf16[32,1536]{1,0:T(8,128)(2,1)S(1)} %constant_dynamic-update-slice_fusion.4.refs_0_), channel_id=1, source_target_pairs={{0,4},{1,5},{2,6},{3,7},{4,0},{5,1},{6,2},{7,3},{8,12},{9,13},{10,... | collective-permute-start | bytes 294920 | tf_op jit(solution)/shard_map/ppermute | solution.py:69
  66.9 1.5 %collective-permute-start.27 = (bf16[32,1536]{1,0:T(8,128)(2,1)S(1)}, bf16[32,1536]{1,0:T(8,128)(2,1)S(1)}, u32[]{:S(2)}, u32[]{:S(2)}) collective-permute-start(bf16[32,1536]{1,0:T(8,128)(2,1)S(1)} %collective-permute-done.23.refs_3_), channel_id=1, source_target_pairs={{0,4},{1,5},{2,6},{3,7},{4,0},{5,1},{6,2},{7,3},{8,12},{9,13},{10,... | collective-permute-start | bytes 294920 | tf_op jit(solution)/shard_map/ppermute | solution.py:69
  67.9 1.3 %collective-permute-start.26 = (bf16[32,1536]{1,0:T(8,128)(2,1)S(1)}, bf16[32,1536]{1,0:T(8,128)(2,1)S(1)}, u32[]{:S(2)}, u32[]{:S(2)}) collective-permute-start(bf16[32,1536]{1,0:T(8,128)(2,1)S(1)} %collective-permute-done.22.refs_2_), channel_id=1, source_target_pairs={{0,4},{1,5},{2,6},{3,7},{4,0},{5,1},{6,2},{7,3},{8,12},{9,13},{10,... | collective-permute-start | bytes 294920 | tf_op jit(solution)/shard_map/ppermute | solution.py:69
  68.3 1.3 %collective-permute-start.25 = (bf16[32,1536]{1,0:T(8,128)(2,1)S(1)}, bf16[32,1536]{1,0:T(8,128)(2,1)S(1)}, u32[]{:S(2)}, u32[]{:S(2)}) collective-permute-start(bf16[32,1536]{1,0:T(8,128)(2,1)S(1)} %collective-permute-done.21.refs_1_), channel_id=1, source_target_pairs={{0,4},{1,5},{2,6},{3,7},{4,0},{5,1},{6,2},{7,3},{8,12},{9,13},{10,... | collective-permute-start | bytes 294920 | tf_op jit(solution)/shard_map/ppermute | solution.py:69
